TPU v7x, 512 devices: a whole 4x8x8 slice. The times are simulated.
512 devices in a mesh: tm: 64 (over x, y, core), dp: 8 (over z).
Axes of the slice: x: 4, y: 8, z: 8, core: 2. Of those that a mesh axis runs over, the one named last changes fastest.
Arguments:
- frame_tokens: bfloat16 [8, 192, 64, 1280], P('dp', 'tm'), may hold values from -8 to 8
- visible: int32 [8, 192, 64], P('dp'), may hold values from 0 to 2
- grad_output: bfloat16 [8, 192, 64, 1280], P('dp', 'tm'), may hold values from -16 to 16
- norm_gain: float32 [1280], replicated, may hold values from 0.1 to 1.9
- query_weight: bfloat16 [1280, 640], P('tm'), may hold values from -1.5 to 1.5
- key_weight: bfloat16 [1280, 640], P('tm'), may hold values from -1.5 to 1.5
- value_weight: bfloat16 [1280, 640], P('tm'), may hold values from -0.15625 to 0.15625
- output_weight: bfloat16 [640, 1280], P('tm'), may hold values from -0.25 to 0.25
Outputs:
- block_out: bfloat16 [8, 192, 64, 1280], P('dp', 'tm')
- grad_tokens: bfloat16 [8, 192, 64, 1280], P('dp', 'tm')
- grad_output_weight: float32 [640, 1280], P('tm')
Inputs may be any that keep to these rules, and one draw needn't show every extreme that they name: visible[c, f, g] names which of the 3 cells of group g is visible in frame f.
All inputs are finite; a program needn't handle non-finite values.
Results may differ from a plain program's by a relative error of at most 0.012.
Values may be sent and summed in bfloat16 or wider, within the bound.
No kernel may reach another device: no remote copies, remote signals or barrier semaphores. Data moves between devices by JAX's collectives and lax.ppermute only.
A program may use at most 64 MiB of HBM per device.

v0:
```python
import math

import jax
import jax.numpy as jnp
from jax import lax
from jax.experimental import pallas as pl
from jax.experimental.pallas import tpu as pltpu
from jax.sharding import Mesh
from jax.sharding import PartitionSpec as P


HEADS = 8
NORM_EPS = 1e-06
PARTS = ("x", "y", "core")
SIZES = (4, 8, 2)


def dot(left, right, contract):
    return lax.dot_general(
        left, right, (contract, ((), ())), preferred_element_type=jnp.float32
    )


NN = ((1,), (0,))
NT = ((1,), (1,))
TN = ((0,), (0,))


def cell_kernel(place_ref, normed_ref, grad_ref, row_ref, col_ref, pick_ref, *rest):
    pieces = rest[:8]
    sent_ref, own_ref, other_ref, out_ref, qkv_ref, whole_ref, arrived = rest[8:]
    low = jnp.bfloat16
    _, lines, depth, _ = whole_ref.shape
    depth //= 2
    copies = []
    for i, piece in enumerate(pieces):
        step = (0, 3, 1, 2)[i % 4]
        at = lax.rem(place_ref[0] + step, 4) * 2 + lax.rem(place_ref[1] + i // 4, 2)
        copies.append(pltpu.make_async_copy(piece, whole_ref.at[at], arrived.at[i]))
    for copy in copies:
        copy.start()
    for copy in copies:
        copy.wait()
    att, _ = out_ref.shape
    size = att // HEADS
    half = depth // 2
    scale = 1.0 / math.sqrt(size)
    for d in range(SIZES[0] * SIZES[1] * SIZES[2]):
        x, y, core = d // (lines * 2), d // 2 % lines, d % 2
        piece = whole_ref.at[x * 2 + core, y]
        qkv_ref[d * depth:(d + 1) * depth, :2 * att] = piece[:depth, :]
        qkv_ref[d * depth:(d + 1) * depth, 2 * att:] = piece[depth:, :att]
        out_ref[d * half:(d + 1) * half, :att] = piece[depth:depth + half, att:]
        out_ref[d * half:(d + 1) * half, att:] = piece[depth + half:, att:]
    qkv = dot(normed_ref[...], qkv_ref[...], NN).astype(low)
    grad_mixed = dot(grad_ref[...], out_ref[...], NT).astype(low)
    same = row_ref[...] == col_ref[...]
    mixed, grad_q, grad_k, grad_v = [], [], [], []
    for h in range(HEADS):
        q = qkv[:, h * size:(h + 1) * size]
        k = qkv[:, att + h * size:att + (h + 1) * size]
        v = qkv[:, 2 * att + h * size:2 * att + (h + 1) * size]
        g = grad_mixed[:, h * size:(h + 1) * size]
        scores = jnp.where(same, dot(q, k, NT) * scale, -jnp.inf)
        expons = jnp.exp(scores - jnp.max(scores, axis=-1, keepdims=True))
        probs = expons / jnp.sum(expons, axis=-1, keepdims=True)
        probs_low = probs.astype(low)
        mixed.append(dot(probs_low, v, NN).astype(low))
        grad_probs = dot(g, v, NT)
        centre = jnp.sum(probs * grad_probs, axis=-1, keepdims=True)
        grad_scores = (probs * (grad_probs - centre) * scale).astype(low)
        grad_q.append(dot(grad_scores, k, NN).astype(low))
        grad_k.append(dot(grad_scores, q, TN).astype(low))
        grad_v.append(dot(probs_low, g, TN).astype(low))
    mixed = jnp.concatenate(mixed, axis=1)
    sent_ref[:, :att] = mixed
    own_ref[...] = dot(mixed, pick_ref[0], NN).astype(low)
    other_ref[...] = dot(mixed, pick_ref[1], NN).astype(low)
    grads = jnp.concatenate(grad_q + grad_k + grad_v, axis=1)
    sent_ref[:, att:] = dot(grads, qkv_ref[...], NT).astype(low)


def cell_part(place, normed, grad, cells, pieces, pick, interpret=False):
    rows, width = normed.shape
    att = pick.shape[1]
    low = jnp.bfloat16
    return pl.pallas_call(
        cell_kernel,
        out_shape=(
            jax.ShapeDtypeStruct((rows, att + width), low),
            jax.ShapeDtypeStruct((rows, att // 2), low),
            jax.ShapeDtypeStruct((rows, att // 2), low),
            jax.ShapeDtypeStruct((att, width), low),
        ),
        in_specs=[pl.BlockSpec(memory_space=pltpu.SMEM)]
        + [pl.BlockSpec(memory_space=pltpu.VMEM)] * 5
        + [pl.BlockSpec(memory_space=pl.ANY)] * len(pieces),
        scratch_shapes=[
            pltpu.VMEM((width, 3 * att), low),
            pltpu.VMEM((SIZES[0] * SIZES[2],) + pieces[0].shape, low),
            pltpu.SemaphoreType.DMA((len(pieces),)),
        ],
        compiler_params=pltpu.CompilerParams(vmem_limit_bytes=56 << 20),
        interpret=interpret,
    )(place, normed, grad, cells[:, None], cells[None, :], pick, *pieces)


def weight_kernel(place_ref, own_ref, got_ref, grad_ref, got_grad_ref, *rest):
    outs, total = rest[:-1], rest[-1]
    total[...] = dot(own_ref[...], grad_ref[...], TN) + dot(
        got_ref[...], got_grad_ref[...], TN
    )
    rows = total.shape[0] // len(outs)
    for k, out in enumerate(outs):
        start = pl.multiple_of(rows * lax.rem(place_ref[0] + k, len(outs)), rows)
        out[...] = total[pl.ds(start, rows), :].astype(out.dtype)


def weight_part(place, own, got, grad, got_grad, interpret=False):
    count = SIZES[0]
    rows, width = own.shape[1] // count, grad.shape[1]
    return pl.pallas_call(
        weight_kernel,
        out_shape=tuple(
            jax.ShapeDtypeStruct((rows, width), jnp.bfloat16 if k else jnp.float32)
            for k in range(count)
        ),
        in_specs=[pl.BlockSpec(memory_space=pltpu.SMEM)]
        + [pl.BlockSpec(memory_space=pltpu.VMEM)] * 4,
        scratch_shapes=[pltpu.VMEM((own.shape[1], width), jnp.float32)],
        compiler_params=pltpu.CompilerParams(vmem_limit_bytes=32 << 20),
        interpret=interpret,
    )(place, own, got, grad, got_grad)


def exchange(values, axis):
    return lax.all_to_all(values, axis, split_axis=0, concat_axis=0, tiled=True)


def shift(values, axis, step, size):
    return lax.ppermute(values, axis, [(i, (i + step) % size) for i in range(size)])


def on_device(frame_tokens, visible, grad_output, norm_gain,
              query_weight, key_weight, value_weight, output_weight):
    low = jnp.bfloat16
    clips = lax.axis_size("dp")
    shards = SIZES[0] * SIZES[1] * SIZES[2]
    tokens = frame_tokens[0]
    frames, _, width = tokens.shape
    _, att = query_weight.shape
    me = lax.axis_index(PARTS)
    core = lax.axis_index("core")

    folded = jnp.concatenate(
        [output_weight[:, :width // 2], output_weight[:, width // 2:]], axis=0
    )
    share = jnp.concatenate(
        [
            jnp.concatenate([query_weight, key_weight], axis=1),
            jnp.concatenate([value_weight, folded], axis=1),
        ],
        axis=0,
    )
    line = exchange(jnp.broadcast_to(share[None], (SIZES[1],) + share.shape), "y")
    left, right = shift(line, "x", 1, SIZES[0]), shift(line, "x", -1, SIZES[0])
    far = shift(right, "x", -1, SIZES[0])
    pieces = (line, left, right, far)
    pieces += tuple(shift(piece, "core", 1, SIZES[2]) for piece in pieces)

    values = tokens.astype(jnp.float32)
    centered = values - jnp.mean(values, axis=-1, keepdims=True)
    inverse = lax.rsqrt(jnp.mean(centered * centered, axis=-1, keepdims=True) + NORM_EPS)
    scaled = centered * inverse
    normed = (scaled * norm_gain).astype(low)

    def to_cells(rows):
        sent = rows.transpose(1, 0, 2).reshape(shards, 2, -1)
        return exchange(sent, PARTS).reshape(shards * frames, -1)

    grad_cells = to_cells(grad_output[0])
    normed_cells = to_cells(normed)
    grad_got = shift(grad_cells, "core", 1, 2)
    cells = lax.dynamic_slice_in_dim(visible[0], me, 1, 1)[:, 0]

    per = att // shards
    column = jnp.arange(att, dtype=jnp.int32)
    x, y = column // (per * 16), column // (per * 2) % 8
    place = (x * 8 + y) * per + column % per
    side = column // per % 2
    at = place[:, None] == jnp.arange(att // 2, dtype=jnp.int32)[None, :]
    pick = jnp.stack(
        [at & (side == core)[:, None], at & (side != core)[:, None]]
    ).astype(low)

    spot = jnp.stack([lax.axis_index("x"), core]).astype(jnp.int32)
    sent, own, other, whole_out = cell_part(
        spot, normed_cells, grad_cells, cells, pieces, pick
    )
    got = shift(other, "core", 1, 2)
    back = exchange(sent.reshape(shards, 2, -1), PARTS)
    rows = back.reshape(shards, frames, att + width).transpose(1, 0, 2)
    mixed, grad_normed = rows[:, :, :att], rows[:, :, att:]

    slabs = weight_part(
        lax.axis_index("x").astype(jnp.int32)[None], own, got, grad_cells, grad_got
    )
    part = slabs[0]
    for k in range(1, SIZES[0]):
        part = part + shift(slabs[k], "x", k, SIZES[0]).astype(jnp.float32)
    part = part.astype(low).reshape(SIZES[1], 2, -1)
    part, _ = lax.optimization_barrier((part, back))
    part = jnp.sum(exchange(part, "y").astype(jnp.float32), axis=0).astype(low)
    part = exchange(jnp.broadcast_to(part[None], (clips,) + part.shape), "dp")
    grad_weight = jnp.sum(part.astype(jnp.float32), axis=0).reshape(per, width)

    flat_mixed = mixed.reshape(-1, att)
    update = jnp.dot(flat_mixed, whole_out, preferred_element_type=jnp.float32)
    block_rows = (values.reshape(-1, width) + update).astype(low).reshape(tokens.shape)
    weighted = grad_normed.astype(jnp.float32) * norm_gain
    first_mean = jnp.mean(weighted, axis=-1, keepdims=True)
    second_mean = jnp.mean(weighted * scaled, axis=-1, keepdims=True)
    grad_rows = inverse * (weighted - first_mean - scaled * second_mean)
    grad_rows = grad_rows + grad_output[0].astype(jnp.float32)
    return (block_rows[None], grad_rows.astype(low)[None], grad_weight)


def solution(mesh):
    fine = Mesh(mesh.devices.reshape(SIZES + (mesh.shape["dp"],)), PARTS + ("dp",))
    rows = P("dp", PARTS, None, None)
    weight = P(PARTS, None)
    return jax.shard_map(
        on_device,
        mesh=fine,
        in_specs=(rows, P("dp", None, None), rows, P(), weight, weight, weight, weight),
        out_specs=(rows, rows, weight),
        check_vma=False,
    )
```

profile of v0, /device:TPU:2, one launch (start us, length us, event | category | flops | bytes accessed | tf_op | source)
XLA Modules:
  0.0 183.3 jit_solution(5603526442359794535)
XLA Ops:
  0.6 0.8 fusion.24
  1.4 0.8 maximum_maximum_fusion
  2.3 30.8 %all_to_all.30.rest_0_ = bf16[8,40,1280]{2,1,0:T(8,128)(2,1)S(1)} all-to-all(bf16[8,40,1280]{2,1,0:T(8,128)(2,1)S(1)} %broadcast_in_dim.6), channel_id=1, replica_groups=mesh['x'=4,'y'=8,'core'=2,'dp'=8] {'y'}, dimensions={0} | all-to-all | bytes 1638400 | tf_op jit(solution)/shard_map/all_to_all | solution.py:137
  33.1 2.4 %collective-permute-start.1 = (bf16[8,40,1280]{2,1,0:T(8,128)(2,1)S(1)}, bf16[8,40,1280]{2,1,0:T(8,128)(2,1)}, u32[]{:S(2)}, u32[]{:S(2)}) collective-permute-start(bf16[8,40,1280]{2,1,0:T(8,128)(2,1)S(1)} %all_to_all.30.rest_0_), channel_id=1, source_target_pairs={{0,384},{128,0},{256,128},{384,256},{1,385},{129,1},{257,129},{385... | collective-permute-start | bytes 2457608 | tf_op jit(solution)/shard_map/ppermute | solution.py:141
  36.0 1.3 reshape.228
  37.4 7.1 %all-to-all-start.1 = ((bf16[64,2,1920]{2,1,0:T(2,128)(2,1)}), bf16[64,2,1920]{2,1,0:T(2,128)(2,1)S(1)}, u32[]{:S(2)}, u32[]{:S(2)}) async-start(bf16[64,2,1920]{2,1,0:T(2,128)(2,1)} %reshape.228), calls=%async_computation.1 | async-start | bytes 983040 | tf_op jit(solution)/shard_map/all_to_all | solution.py:137
  44.9 0.6 multiply_reduce_fusion.1
  45.5 3.5 %collective-permute-start = (bf16[8,40,1280]{2,1,0:T(8,128)(2,1)S(1)}, bf16[8,40,1280]{2,1,0:T(8,128)(2,1)}, u32[]{:S(2)}, u32[]{:S(2)}) collective-permute-start(bf16[8,40,1280]{2,1,0:T(8,128)(2,1)S(1)} %all_to_all.30.rest_0_), channel_id=1, source_target_pairs={{0,128},{128,256},{256,384},{384,0},{1,129},{129,257},{257,385},{3... | collective-permute-start | bytes 2457608 | tf_op jit(solution)/shard_map/ppermute | solution.py:141
  49.0 8.8 %collective-permute-done.1.rest_2_ = bf16[8,40,1280]{2,1,0:T(8,128)(2,1)} collective-permute-done((bf16[8,40,1280]{2,1,0:T(8,128)(2,1)S(1)}, bf16[8,40,1280]{2,1,0:T(8,128)(2,1)}, u32[]{:S(2)}, u32[]{:S(2)}) %collective-permute-start.1) | collective-permute-done | bytes 819232 | tf_op jit(solution)/shard_map/ppermute | solution.py:141
  57.8 3.2 %collective-permute-start.2 = (bf16[8,40,1280]{2,1,0:T(8,128)(2,1)}, bf16[8,40,1280]{2,1,0:T(8,128)(2,1)}, u32[]{:S(2)}, u32[]{:S(2)}) collective-permute-start(bf16[8,40,1280]{2,1,0:T(8,128)(2,1)} %collective-permute-done.1.rest_2_), channel_id=1, source_target_pairs={{0,384},{128,0},{256,128},{384,256},{1,385},{129,1},{257,129},{385... | collective-permute-start | bytes 2457608 | tf_op jit(solution)/shard_map/ppermute | solution.py:141
  61.1 0.6 fusion.5
  61.7 1.3 reshape.226
  63.0 7.9 %all-to-all-start = ((bf16[64,2,1920]{2,1,0:T(2,128)(2,1)}), bf16[64,2,1920]{2,1,0:T(2,128)(2,1)S(1)}, u32[]{:S(2)}, u32[]{:S(2)}) async-start(bf16[64,2,1920]{2,1,0:T(2,128)(2,1)} %reshape.226), calls=%async_computation | async-start | bytes 983040 | tf_op jit(solution)/shard_map/all_to_all | solution.py:137
  71.0 2.0 %collective-permute-start.3 = (bf16[8,40,1280]{2,1,0:T(8,128)(2,1)S(1)}, bf16[8,40,1280]{2,1,0:T(8,128)(2,1)}, u32[]{:S(2)}, u32[]{:S(2)}) collective-permute-start(bf16[8,40,1280]{2,1,0:T(8,128)(2,1)S(1)} %all_to_all.30.rest_0_), channel_id=1, source_target_pairs={{0,8},{8,0},{1,9},{9,1},{2,10},{10,2},{3,11},{11,3},{4,12},{12,4},... | collective-permute-start | bytes 2457608 | tf_op jit(solution)/shard_map/ppermute | solution.py:141
  73.0 2.3 %collective-permute-start.5 = (bf16[8,40,1280]{2,1,0:T(8,128)(2,1)}, bf16[8,40,1280]{2,1,0:T(8,128)(2,1)}, u32[]{:S(2)}, u32[]{:S(2)}) collective-permute-start(bf16[8,40,1280]{2,1,0:T(8,128)(2,1)} %collective-permute-done.1.rest_2_), channel_id=1, source_target_pairs={{0,8},{8,0},{1,9},{9,1},{2,10},{10,2},{3,11},{11,3},{4,12},{12,4},... | collective-permute-start | bytes 2457608 | tf_op jit(solution)/shard_map/ppermute | solution.py:141
  75.3 2.0 %collective-permute-start.4 = (bf16[8,40,1280]{2,1,0:T(8,128)(2,1)}, bf16[8,40,1280]{2,1,0:T(8,128)(2,1)}, u32[]{:S(2)}, u32[]{:S(2)}) collective-permute-start(bf16[8,40,1280]{2,1,0:T(8,128)(2,1)} %collective-permute-done.rest_1_), channel_id=1, source_target_pairs={{0,8},{8,0},{1,9},{9,1},{2,10},{10,2},{3,11},{11,3},{4,12},{12,4},... | collective-permute-start | bytes 2457608 | tf_op jit(solution)/shard_map/ppermute | solution.py:141
  77.4 2.3 %collective-permute-start.6 = (bf16[8,40,1280]{2,1,0:T(8,128)(2,1)}, bf16[8,40,1280]{2,1,0:T(8,128)(2,1)}, u32[]{:S(2)}, u32[]{:S(2)}) collective-permute-start(bf16[8,40,1280]{2,1,0:T(8,128)(2,1)} %collective-permute-done.2.rest_3_), channel_id=1, source_target_pairs={{0,8},{8,0},{1,9},{9,1},{2,10},{10,2},{3,11},{11,3},{4,12},{12,4},... | collective-permute-start | bytes 2457608 | tf_op jit(solution)/shard_map/ppermute | solution.py:141
  79.7 1.3 dynamic-slice_bitcast_fusion
  81.0 0.8 copy.38.row_ref
  82.1 1.2 add_convert_fusion.pick_ref
  83.3 1.1 reshape.229.grad_ref
  84.4 2.2 %collective-permute-start.8 = (bf16[192,1280]{1,0:T(8,128)(2,1)}, bf16[192,1280]{1,0:T(8,128)(2,1)S(1)}, u32[]{:S(2)}, u32[]{:S(2)}) collective-permute-start(bf16[192,1280]{1,0:T(8,128)(2,1)} %reshape.229.grad_ref), channel_id=1, source_target_pairs={{0,8},{8,0},{1,9},{9,1},{2,10},{10,2},{3,11},{11,3},{4,12},{12,4},... | collective-permute-start | bytes 1474568 | tf_op jit(solution)/shard_map/ppermute | solution.py:141
  86.6 0.6 pad_add_fusion.place_ref
  87.2 1.1 reshape.227.normed_ref
  88.3 13.4 %shard_map.103 = (bf16[192,1920]{1,0:T(8,128)(2,1)}, bf16[192,320]{1,0:T(8,128)(2,1)}, bf16[192,320]{1,0:T(8,128)(2,1)}, bf16[640,1280]{1,0:T(8,128)(2,1)}) custom-call(s32[2]{0:T(128)} %pad_add_fusion.place_ref, bf16[192,1280]{1,0:T(8,128)(2,1)} %reshape.227.normed_ref, bf16[192,1280]{1,0:T(8,128)(2,1)} %reshape.229.grad_ref, s32[192,1]{1,0:T(8,128)} %copy.38.row_ref, ...), custom_call_target="tpu_custom_call" | custom-call | tf_op jit(solution)/shard_map/pallas_call | solution.py:87
  101.7 3.4 %reshape.230 = bf16[64,2,2880]{2,1,0:T(2,128)(2,1)} reshape(bf16[192,1920]{1,0:T(8,128)(2,1)} %get-tuple-element.12) | data formatting | bytes 1474560 | tf_op jit(solution)/shard_map/reshape | solution.py:201
  105.1 13.8 %all-to-all-start.3 = ((bf16[64,2,2880]{2,1,0:T(2,128)(2,1)}), bf16[64,2,2880]{2,1,0:T(2,128)(2,1)S(1)}, u32[]{:S(2)}, u32[]{:S(2)}) async-start(bf16[64,2,2880]{2,1,0:T(2,128)(2,1)} %reshape.230), calls=%async_computation.3 | async-start | bytes 1507328 | tf_op jit(solution)/shard_map/all_to_all | solution.py:137
  118.9 2.0 %collective-permute-start.7 = (bf16[192,320]{1,0:T(8,128)(2,1)S(1)}, bf16[192,320]{1,0:T(8,128)(2,1)S(1)}, u32[]{:S(2)}, u32[]{:S(2)}) collective-permute-start(bf16[192,320]{1,0:T(8,128)(2,1)S(1)} %copy-done.6), channel_id=1, source_target_pairs={{0,8},{8,0},{1,9},{9,1},{2,10},{10,2},{3,11},{11,3},{4,12},{12,4},... | collective-permute-start | bytes 368648 | tf_op jit(solution)/shard_map/ppermute | solution.py:141
  120.9 1.2 collective-permute-done.7.got_ref
  122.1 1.8 shard_map.104
  123.9 4.2 %collective-permute-start.10 = (bf16[80,1280]{1,0:T(8,128)(2,1)S(1)}, bf16[80,1280]{1,0:T(8,128)(2,1)S(1)}, u32[]{:S(2)}, u32[]{:S(2)}) collective-permute-start(bf16[80,1280]{1,0:T(8,128)(2,1)S(1)} %get-tuple-element.18), channel_id=1, source_target_pairs={{0,256},{128,384},{256,0},{384,128},{1,257},{129,385},{257,1},{385... | collective-permute-start | bytes 614408 | tf_op jit(solution)/shard_map/ppermute | solution.py:141
  128.1 3.3 %collective-permute-start.11 = (bf16[80,1280]{1,0:T(8,128)(2,1)S(1)}, bf16[80,1280]{1,0:T(8,128)(2,1)S(1)}, u32[]{:S(2)}, u32[]{:S(2)}) collective-permute-start(bf16[80,1280]{1,0:T(8,128)(2,1)S(1)} %get-tuple-element.19), channel_id=1, source_target_pairs={{0,384},{128,0},{256,128},{384,256},{1,385},{129,1},{257,129},{385... | collective-permute-start | bytes 614408 | tf_op jit(solution)/shard_map/ppermute | solution.py:141
  131.4 2.6 %collective-permute-start.9 = (bf16[80,1280]{1,0:T(8,128)(2,1)S(1)}, bf16[80,1280]{1,0:T(8,128)(2,1)S(1)}, u32[]{:S(2)}, u32[]{:S(2)}) collective-permute-start(bf16[80,1280]{1,0:T(8,128)(2,1)S(1)} %get-tuple-element.17), channel_id=1, source_target_pairs={{0,128},{128,256},{256,384},{384,0},{1,129},{129,257},{257,385},{3... | collective-permute-start | bytes 614408 | tf_op jit(solution)/shard_map/ppermute | solution.py:141
  134.6 4.7 %collective-permute-done.10 = bf16[80,1280]{1,0:T(8,128)(2,1)S(1)} collective-permute-done((bf16[80,1280]{1,0:T(8,128)(2,1)S(1)}, bf16[80,1280]{1,0:T(8,128)(2,1)S(1)}, u32[]{:S(2)}, u32[]{:S(2)}) %collective-permute-start.10) | collective-permute-done | bytes 204832 | tf_op jit(solution)/shard_map/ppermute | solution.py:141
  139.3 4.2 %collective-permute-done.11 = bf16[80,1280]{1,0:T(8,128)(2,1)S(1)} collective-permute-done((bf16[80,1280]{1,0:T(8,128)(2,1)S(1)}, bf16[80,1280]{1,0:T(8,128)(2,1)S(1)}, u32[]{:S(2)}, u32[]{:S(2)}) %collective-permute-start.11) | collective-permute-done | bytes 204832 | tf_op jit(solution)/shard_map/ppermute | solution.py:141
  143.5 0.8 reshape.233
  144.3 6.3 %all-to-all-start.4 = ((bf16[8,2,6400]{2,1,0:T(2,128)(2,1)}), bf16[8,2,6400]{2,1,0:T(2,128)(2,1)S(1)}, u32[]{:S(2)}, u32[]{:S(2)}) async-start(bf16[8,2,6400]{2,1,0:T(2,128)(2,1)} %reshape.233), calls=%async_computation.4 | async-start | bytes 409600 | tf_op jit(solution)/shard_map/all_to_all | solution.py:137
  150.6 1.1 reshape.231
  151.7 1.1 fusion.1
  152.8 8.7 %all-to-all-done.4 = bf16[8,2,6400]{2,1,0:T(2,128)(2,1)S(1)} async-done(((bf16[8,2,6400]{2,1,0:T(2,128)(2,1)}), bf16[8,2,6400]{2,1,0:T(2,128)(2,1)S(1)}, u32[]{:S(2)}, u32[]{:S(2)}) %all-to-all-start.4) | async-done | bytes 204832 | tf_op jit(solution)/shard_map/all_to_all | solution.py:137
  161.7 0.8 broadcast_in_dim.8
  162.4 10.2 %all-to-all-start.5 = ((bf16[8,2,6400]{2,1,0:T(2,128)(2,1)}), bf16[8,2,6400]{2,1,0:T(2,128)(2,1)S(1)}, u32[]{:S(2)}, u32[]{:S(2)}) async-start(bf16[8,2,6400]{2,1,0:T(2,128)(2,1)} %broadcast_in_dim.8), calls=%async_computation.5 | async-start | bytes 409600 | tf_op jit(solution)/shard_map/all_to_all | solution.py:137
  172.6 2.6 %fusion.6 = bf16[1,3,64,1280]{3,1,2,0:T(4,128)(2,1)S(1)} fusion(f32[3,64]{0,1:T(8,128)S(1)} %broadcast_multiply_fusion, f32[3,64]{0,1:T(8,128)S(1)} %broadcast_multiply_fusion.2, f32[3,64]{0,1:T(8,128)S(1)} %broadcast_multiply_fusion.1, f32[1280]{0:T(1024)S(1)} %copy-done.5, f32[3,64]{0,1:T(8,128)S(1)} %add_rsqrt_fusion, bf16[1,3,64,1280]{3,2,1,0:T(8,128)(2,1)} %param.10, ...), kind=kLoop, calls=%fused_computation.16 | loop fusion | flops 2949120 | bytes 1974272 | tf_op jit(solution)/shard_map/broadcast_in_dim | solution.py:225
  175.4 0.8 copy.41
  176.2 0.6 copy-done.4
  176.9 1.3 fusion
  178.2 4.3 %all-to-all-done.5 = bf16[8,2,6400]{2,1,0:T(2,128)(2,1)S(1)} async-done(((bf16[8,2,6400]{2,1,0:T(2,128)(2,1)}), bf16[8,2,6400]{2,1,0:T(2,128)(2,1)S(1)}, u32[]{:S(2)}, u32[]{:S(2)}) %all-to-all-start.5) | async-done | bytes 204832 | tf_op jit(solution)/shard_map/all_to_all | solution.py:137
  182.6 0.7 reshape.234
  (41 shorter events, 2.6 us)
Async XLA Ops:
  2.2 33.4 %copy-start.3 = (bf16[1,3,64,1280]{3,2,1,0:T(8,128)(2,1)S(1)}, bf16[1,3,64,1280]{3,2,1,0:T(8,128)(2,1)}, u32[]{:S(2)}) copy-start(bf16[1,3,64,1280]{3,2,1,0:T(8,128)(2,1)} %param.10) | copy-start | bytes 1474564
  33.1 37.8 %copy-start.2 = (bf16[8,40,1280]{2,1,0:T(8,128)(2,1)}, bf16[8,40,1280]{2,1,0:T(8,128)(2,1)S(1)}, u32[]{:S(2)}) copy-start(bf16[8,40,1280]{2,1,0:T(8,128)(2,1)S(1)} %all_to_all.30.rest_0_) | copy-start | bytes 2457604
  33.1 24.7 %collective-permute-start.1 = (bf16[8,40,1280]{2,1,0:T(8,128)(2,1)S(1)}, bf16[8,40,1280]{2,1,0:T(8,128)(2,1)}, u32[]{:S(2)}, u32[]{:S(2)}) collective-permute-start(bf16[8,40,1280]{2,1,0:T(8,128)(2,1)S(1)} %all_to_all.30.rest_0_), channel_id=1, source_target_pairs={{0,384},{128,0},{256,128},{384,256},{1,385},{129,1},{257,129},{385... | collective-permute-start | bytes 2457608 | tf_op jit(solution)/shard_map/ppermute | solution.py:141
  36.0 8.4 %copy-start.1 = (bf16[1,3,64,1280]{3,2,1,0:T(8,128)(2,1)S(1)}, bf16[1,3,64,1280]{3,2,1,0:T(8,128)(2,1)}, u32[]{:S(2)}) copy-start(bf16[1,3,64,1280]{3,2,1,0:T(8,128)(2,1)} %param.8) | copy-start | bytes 1474564
  37.4 23.7 %copy-start.5 = (f32[1280]{0:T(1024)S(1)}, f32[1280]{0:T(1024)}, u32[]{:S(2)}) copy-start(f32[1280]{0:T(1024)} %param.11) | copy-start | bytes 15364
  37.4 25.7 %all-to-all-start.1 = ((bf16[64,2,1920]{2,1,0:T(2,128)(2,1)}), bf16[64,2,1920]{2,1,0:T(2,128)(2,1)S(1)}, u32[]{:S(2)}, u32[]{:S(2)}) async-start(bf16[64,2,1920]{2,1,0:T(2,128)(2,1)} %reshape.228), calls=%async_computation.1 | async-start | bytes 983040 | tf_op jit(solution)/shard_map/all_to_all | solution.py:137
  45.5 29.8 %collective-permute-start = (bf16[8,40,1280]{2,1,0:T(8,128)(2,1)S(1)}, bf16[8,40,1280]{2,1,0:T(8,128)(2,1)}, u32[]{:S(2)}, u32[]{:S(2)}) collective-permute-start(bf16[8,40,1280]{2,1,0:T(8,128)(2,1)S(1)} %all_to_all.30.rest_0_), channel_id=1, source_target_pairs={{0,128},{128,256},{256,384},{384,0},{1,129},{129,257},{257,385},{3... | collective-permute-start | bytes 2457608 | tf_op jit(solution)/shard_map/ppermute | solution.py:141
  57.8 19.6 %collective-permute-start.2 = (bf16[8,40,1280]{2,1,0:T(8,128)(2,1)}, bf16[8,40,1280]{2,1,0:T(8,128)(2,1)}, u32[]{:S(2)}, u32[]{:S(2)}) collective-permute-start(bf16[8,40,1280]{2,1,0:T(8,128)(2,1)} %collective-permute-done.1.rest_2_), channel_id=1, source_target_pairs={{0,384},{128,0},{256,128},{384,256},{1,385},{129,1},{257,129},{385... | collective-permute-start | bytes 2457608 | tf_op jit(solution)/shard_map/ppermute | solution.py:141
  63.0 24.2 %all-to-all-start = ((bf16[64,2,1920]{2,1,0:T(2,128)(2,1)}), bf16[64,2,1920]{2,1,0:T(2,128)(2,1)S(1)}, u32[]{:S(2)}, u32[]{:S(2)}) async-start(bf16[64,2,1920]{2,1,0:T(2,128)(2,1)} %reshape.226), calls=%async_computation | async-start | bytes 983040 | tf_op jit(solution)/shard_map/all_to_all | solution.py:137
  71.0 17.3 %collective-permute-start.3 = (bf16[8,40,1280]{2,1,0:T(8,128)(2,1)S(1)}, bf16[8,40,1280]{2,1,0:T(8,128)(2,1)}, u32[]{:S(2)}, u32[]{:S(2)}) collective-permute-start(bf16[8,40,1280]{2,1,0:T(8,128)(2,1)S(1)} %all_to_all.30.rest_0_), channel_id=1, source_target_pairs={{0,8},{8,0},{1,9},{9,1},{2,10},{10,2},{3,11},{11,3},{4,12},{12,4},... | collective-permute-start | bytes 2457608 | tf_op jit(solution)/shard_map/ppermute | solution.py:141
  73.0 15.3 %collective-permute-start.5 = (bf16[8,40,1280]{2,1,0:T(8,128)(2,1)}, bf16[8,40,1280]{2,1,0:T(8,128)(2,1)}, u32[]{:S(2)}, u32[]{:S(2)}) collective-permute-start(bf16[8,40,1280]{2,1,0:T(8,128)(2,1)} %collective-permute-done.1.rest_2_), channel_id=1, source_target_pairs={{0,8},{8,0},{1,9},{9,1},{2,10},{10,2},{3,11},{11,3},{4,12},{12,4},... | collective-permute-start | bytes 2457608 | tf_op jit(solution)/shard_map/ppermute | solution.py:141
  75.3 13.0 %collective-permute-start.4 = (bf16[8,40,1280]{2,1,0:T(8,128)(2,1)}, bf16[8,40,1280]{2,1,0:T(8,128)(2,1)}, u32[]{:S(2)}, u32[]{:S(2)}) collective-permute-start(bf16[8,40,1280]{2,1,0:T(8,128)(2,1)} %collective-permute-done.rest_1_), channel_id=1, source_target_pairs={{0,8},{8,0},{1,9},{9,1},{2,10},{10,2},{3,11},{11,3},{4,12},{12,4},... | collective-permute-start | bytes 2457608 | tf_op jit(solution)/shard_map/ppermute | solution.py:141
  77.4 10.9 %collective-permute-start.6 = (bf16[8,40,1280]{2,1,0:T(8,128)(2,1)}, bf16[8,40,1280]{2,1,0:T(8,128)(2,1)}, u32[]{:S(2)}, u32[]{:S(2)}) collective-permute-start(bf16[8,40,1280]{2,1,0:T(8,128)(2,1)} %collective-permute-done.2.rest_3_), channel_id=1, source_target_pairs={{0,8},{8,0},{1,9},{9,1},{2,10},{10,2},{3,11},{11,3},{4,12},{12,4},... | collective-permute-start | bytes 2457608 | tf_op jit(solution)/shard_map/ppermute | solution.py:141
  84.4 36.5 %collective-permute-start.8 = (bf16[192,1280]{1,0:T(8,128)(2,1)}, bf16[192,1280]{1,0:T(8,128)(2,1)S(1)}, u32[]{:S(2)}, u32[]{:S(2)}) collective-permute-start(bf16[192,1280]{1,0:T(8,128)(2,1)} %reshape.229.grad_ref), channel_id=1, source_target_pairs={{0,8},{8,0},{1,9},{9,1},{2,10},{10,2},{3,11},{11,3},{4,12},{12,4},... | collective-permute-start | bytes 1474568 | tf_op jit(solution)/shard_map/ppermute | solution.py:141
  101.7 17.2 %copy-start.6 = (bf16[192,320]{1,0:T(8,128)(2,1)S(1)}, bf16[192,320]{1,0:T(8,128)(2,1)}, u32[]{:S(2)}) copy-start(bf16[192,320]{1,0:T(8,128)(2,1)} %get-tuple-element.15) | copy-start | bytes 368644
  101.7 20.4 %copy-start = (bf16[192,320]{1,0:T(8,128)(2,1)S(1)}, bf16[192,320]{1,0:T(8,128)(2,1)}, u32[]{:S(2)}) copy-start(bf16[192,320]{1,0:T(8,128)(2,1)} %get-tuple-element.14.own_ref) | copy-start | bytes 368644
  105.1 39.2 %all-to-all-start.3 = ((bf16[64,2,2880]{2,1,0:T(2,128)(2,1)}), bf16[64,2,2880]{2,1,0:T(2,128)(2,1)S(1)}, u32[]{:S(2)}, u32[]{:S(2)}) async-start(bf16[64,2,2880]{2,1,0:T(2,128)(2,1)} %reshape.230), calls=%async_computation.3 | async-start | bytes 1507328 | tf_op jit(solution)/shard_map/all_to_all | solution.py:137
  118.9 3.3 %collective-permute-start.7 = (bf16[192,320]{1,0:T(8,128)(2,1)S(1)}, bf16[192,320]{1,0:T(8,128)(2,1)S(1)}, u32[]{:S(2)}, u32[]{:S(2)}) collective-permute-start(bf16[192,320]{1,0:T(8,128)(2,1)S(1)} %copy-done.6), channel_id=1, source_target_pairs={{0,8},{8,0},{1,9},{9,1},{2,10},{10,2},{3,11},{11,3},{4,12},{12,4},... | collective-permute-start | bytes 368648 | tf_op jit(solution)/shard_map/ppermute | solution.py:141
  123.9 15.3 %collective-permute-start.10 = (bf16[80,1280]{1,0:T(8,128)(2,1)S(1)}, bf16[80,1280]{1,0:T(8,128)(2,1)S(1)}, u32[]{:S(2)}, u32[]{:S(2)}) collective-permute-start(bf16[80,1280]{1,0:T(8,128)(2,1)S(1)} %get-tuple-element.18), channel_id=1, source_target_pairs={{0,256},{128,384},{256,0},{384,128},{1,257},{129,385},{257,1},{385... | collective-permute-start | bytes 614408 | tf_op jit(solution)/shard_map/ppermute | solution.py:141
  128.1 15.3 %collective-permute-start.11 = (bf16[80,1280]{1,0:T(8,128)(2,1)S(1)}, bf16[80,1280]{1,0:T(8,128)(2,1)S(1)}, u32[]{:S(2)}, u32[]{:S(2)}) collective-permute-start(bf16[80,1280]{1,0:T(8,128)(2,1)S(1)} %get-tuple-element.19), channel_id=1, source_target_pairs={{0,384},{128,0},{256,128},{384,256},{1,385},{129,1},{257,129},{385... | collective-permute-start | bytes 614408 | tf_op jit(solution)/shard_map/ppermute | solution.py:141
  131.4 12.1 %collective-permute-start.9 = (bf16[80,1280]{1,0:T(8,128)(2,1)S(1)}, bf16[80,1280]{1,0:T(8,128)(2,1)S(1)}, u32[]{:S(2)}, u32[]{:S(2)}) collective-permute-start(bf16[80,1280]{1,0:T(8,128)(2,1)S(1)} %get-tuple-element.17), channel_id=1, source_target_pairs={{0,128},{128,256},{256,384},{384,0},{1,129},{129,257},{257,385},{3... | collective-permute-start | bytes 614408 | tf_op jit(solution)/shard_map/ppermute | solution.py:141
  144.3 17.2 %all-to-all-start.4 = ((bf16[8,2,6400]{2,1,0:T(2,128)(2,1)}), bf16[8,2,6400]{2,1,0:T(2,128)(2,1)S(1)}, u32[]{:S(2)}, u32[]{:S(2)}) async-start(bf16[8,2,6400]{2,1,0:T(2,128)(2,1)} %reshape.233), calls=%async_computation.4 | async-start | bytes 409600 | tf_op jit(solution)/shard_map/all_to_all | solution.py:137
  162.4 20.0 %all-to-all-start.5 = ((bf16[8,2,6400]{2,1,0:T(2,128)(2,1)}), bf16[8,2,6400]{2,1,0:T(2,128)(2,1)S(1)}, u32[]{:S(2)}, u32[]{:S(2)}) async-start(bf16[8,2,6400]{2,1,0:T(2,128)(2,1)} %broadcast_in_dim.8), calls=%async_computation.5 | async-start | bytes 409600 | tf_op jit(solution)/shard_map/all_to_all | solution.py:137
  175.2 1.6 copy-start.4
where the time goes:
time: 185 us; the launch traced here: 183 us
  starting transfers between devices  77.3 us (42%)
  waiting for transfers between devices  31.9 us (17%)
  blocking collectives  30.8 us (17%)
  local copies, waits for them, and re-layouts  16.6 us (9%)
  Pallas kernels  15.2 us (8%)
  other arithmetic  9.23 us (5%)
    all_to_all x5, starting transfers between devices, exchange(): return lax.all_to_all(values, axis, split_axis=0, concat_axis=0, tiled=True)  45.3 us
    ppermute x12, starting transfers between devices, shift(): lax.ppermute(values, axis, [(i, (i + step) % size) for i in range(size)])  32 us
    all_to_all x1, blocking collectives, exchange(): return lax.all_to_all(values, axis, split_axis=0, concat_axis=0, tiled=True)  30.8 us
    ppermute x12, waiting for transfers between devices, shift(): lax.ppermute(values, axis, [(i, (i + step) % size) for i in range(size)])  18.9 us
    pallas_call x1, Pallas kernels, cell_part(): pl.pallas_call(cell_kernel, out_shape=(jax.ShapeDtypeStruct((rows, att +...  13.4 us
    all_to_all x5, waiting for transfers between devices, exchange(): return lax.all_to_all(values, axis, split_axis=0, concat_axis=0, tiled=True)  13 us
  transfers between devices with their start and end apart: 17, of which 6 were waited for; matrix products, arithmetic and copies ran while one was open for 13% of the time, Pallas kernels for 8%

commit v1 on v0

--- a/solution.py
+++ b/solution.py
@@ -133,6 +133,37 @@
     )(place, own, got, grad, got_grad)
 
 
+def spread_kernel(place_ref, stay_ref, *rest):
+    count = SIZES[1]
+    came, outs = rest[:-count], rest[-count:]
+    total = stay_ref[...]
+    for piece in came:
+        total = total + piece[...].astype(jnp.float32)
+    rows = total.shape[0] // count
+    for place in range(count):
+        @pl.when(place_ref[0] == place)
+        def _():
+            for k, out in enumerate(outs):
+                start = rows * ((place + k) % count)
+                out[...] = total[start:start + rows].astype(out.dtype)
+
+
+def spread(place, stay, came, interpret=False):
+    count = SIZES[1]
+    rows, width = stay.shape[0] // count, stay.shape[1]
+    return pl.pallas_call(
+        spread_kernel,
+        out_shape=tuple(
+            jax.ShapeDtypeStruct((rows, width), jnp.bfloat16 if k else jnp.float32)
+            for k in range(count)
+        ),
+        in_specs=[pl.BlockSpec(memory_space=pltpu.SMEM)]
+        + [pl.BlockSpec(memory_space=pltpu.VMEM)] * (1 + len(came)),
+        compiler_params=pltpu.CompilerParams(vmem_limit_bytes=32 << 20),
+        interpret=interpret,
+    )(place, stay, *came)
+
+
 def exchange(values, axis):
     return lax.all_to_all(values, axis, split_axis=0, concat_axis=0, tiled=True)
 
@@ -165,8 +196,9 @@
     line = exchange(jnp.broadcast_to(share[None], (SIZES[1],) + share.shape), "y")
     left, right = shift(line, "x", 1, SIZES[0]), shift(line, "x", -1, SIZES[0])
     far = shift(right, "x", -1, SIZES[0])
-    pieces = (line, left, right, far)
-    pieces += tuple(shift(piece, "core", 1, SIZES[2]) for piece in pieces)
+    line_other = shift(line, "core", 1, SIZES[2])
+    pieces = (line, left, right, far, line_other)
+    pieces += tuple(shift(piece, "core", 1, SIZES[2]) for piece in (left, right, far))
 
     values = tokens.astype(jnp.float32)
     centered = values - jnp.mean(values, axis=-1, keepdims=True)
@@ -205,12 +237,12 @@
     slabs = weight_part(
         lax.axis_index("x").astype(jnp.int32)[None], own, got, grad_cells, grad_got
     )
+    came = [shift(slabs[k], "x", k, SIZES[0]) for k in range(1, SIZES[0])]
+    slabs = spread(lax.axis_index("y").astype(jnp.int32)[None], slabs[0], came)
     part = slabs[0]
-    for k in range(1, SIZES[0]):
-        part = part + shift(slabs[k], "x", k, SIZES[0]).astype(jnp.float32)
-    part = part.astype(low).reshape(SIZES[1], 2, -1)
-    part, _ = lax.optimization_barrier((part, back))
-    part = jnp.sum(exchange(part, "y").astype(jnp.float32), axis=0).astype(low)
+    for k in range(1, SIZES[1]):
+        part = part + shift(slabs[k], "y", k, SIZES[1]).astype(jnp.float32)
+    part, _ = lax.optimization_barrier((part.astype(low).reshape(2, -1), back))
     part = exchange(jnp.broadcast_to(part[None], (clips,) + part.shape), "dp")
     grad_weight = jnp.sum(part.astype(jnp.float32), axis=0).reshape(per, width)
 

time: 185 us -> 199 us (1.076)
  starting transfers between devices: 77.3 us -> 101 us
  waiting for transfers between devices: 31.9 us -> 24 us
    ppermute x12 -> x19, starting transfers between devices: 32 us -> 61.9 us  [shift(): lax.ppermute(values, axis, [(i, (i + step) % size) for i in range(size)])]
    all_to_all x5 -> x4, waiting for transfers between devices: 13 us -> 2.73 us  [exchange(): return lax.all_to_all(values, axis, split_axis=0, concat_axis=0, tiled=True)]
    all_to_all x5 -> x4, starting transfers between devices: 45.3 us -> 38.9 us  [exchange(): return lax.all_to_all(values, axis, split_axis=0, concat_axis=0, tiled=True)]
    ppermute x12 -> x19, waiting for transfers between devices: 18.9 us -> 21.3 us  [shift(): lax.ppermute(values, axis, [(i, (i + step) % size) for i in range(size)])]
  transfers between devices with their start and end apart: 17 -> 23, of which waited for: 6 -> 6; matrix products, arithmetic and copies ran while one was open for 13% -> 11% of each run, Pallas kernels for 8% -> 8%
where the time goes in v1:
time: 199 us; the launch traced here: 198 us
  starting transfers between devices  101 us (51%)
  blocking collectives  30.8 us (15%)
  waiting for transfers between devices  24 us (12%)
  local copies, waits for them, and re-layouts  15.9 us (8%)
  Pallas kernels  15.4 us (8%)
  other arithmetic  8.37 us (4%)
    ppermute x19, starting transfers between devices, shift(): lax.ppermute(values, axis, [(i, (i + step) % size) for i in range(size)])  61.9 us
    all_to_all x4, starting transfers between devices, exchange(): return lax.all_to_all(values, axis, split_axis=0, concat_axis=0, tiled=True)  38.9 us
    all_to_all x1, blocking collectives, exchange(): return lax.all_to_all(values, axis, split_axis=0, concat_axis=0, tiled=True)  30.8 us
    ppermute x19, waiting for transfers between devices, shift(): lax.ppermute(values, axis, [(i, (i + step) % size) for i in range(size)])  21.3 us
    pallas_call x1, Pallas kernels, cell_part(): pl.pallas_call(cell_kernel, out_shape=(jax.ShapeDtypeStruct((rows, att +...  13.4 us
  transfers between devices with their start and end apart: 23, of which 6 were waited for; matrix products, arithmetic and copies ran while one was open for 11% of the time, Pallas kernels for 8%

profile of v1, /device:TPU:2, one launch (start us, length us, event | category | flops | bytes accessed | tf_op | source)
XLA Modules:
  0.0 197.8 jit_solution(12917220293555838730)
XLA Ops:
  0.6 0.8 fusion.24
  1.4 0.8 maximum_maximum_fusion
  2.3 30.8 %all_to_all.25.rest_0_ = bf16[8,40,1280]{2,1,0:T(8,128)(2,1)S(1)} all-to-all(bf16[8,40,1280]{2,1,0:T(8,128)(2,1)S(1)} %broadcast_in_dim.8), channel_id=1, replica_groups=mesh['x'=4,'y'=8,'core'=2,'dp'=8] {'y'}, dimensions={0} | all-to-all | bytes 1638400 | tf_op jit(solution)/shard_map/all_to_all | solution.py:168
  33.1 2.4 %collective-permute-start.1 = (bf16[8,40,1280]{2,1,0:T(8,128)(2,1)S(1)}, bf16[8,40,1280]{2,1,0:T(8,128)(2,1)}, u32[]{:S(2)}, u32[]{:S(2)}) collective-permute-start(bf16[8,40,1280]{2,1,0:T(8,128)(2,1)S(1)} %all_to_all.25.rest_0_), channel_id=1, source_target_pairs={{0,384},{128,0},{256,128},{384,256},{1,385},{129,1},{257,129},{385... | collective-permute-start | bytes 2457608 | tf_op jit(solution)/shard_map/ppermute | solution.py:172
  36.0 1.3 reshape.228
  37.4 7.1 %all-to-all-start.1 = ((bf16[64,2,1920]{2,1,0:T(2,128)(2,1)}), bf16[64,2,1920]{2,1,0:T(2,128)(2,1)S(1)}, u32[]{:S(2)}, u32[]{:S(2)}) async-start(bf16[64,2,1920]{2,1,0:T(2,128)(2,1)} %reshape.228), calls=%async_computation.1 | async-start | bytes 983040 | tf_op jit(solution)/shard_map/all_to_all | solution.py:168
  45.5 3.5 %collective-permute-start = (bf16[8,40,1280]{2,1,0:T(8,128)(2,1)S(1)}, bf16[8,40,1280]{2,1,0:T(8,128)(2,1)}, u32[]{:S(2)}, u32[]{:S(2)}) collective-permute-start(bf16[8,40,1280]{2,1,0:T(8,128)(2,1)S(1)} %all_to_all.25.rest_0_), channel_id=1, source_target_pairs={{0,128},{128,256},{256,384},{384,0},{1,129},{129,257},{257,385},{3... | collective-permute-start | bytes 2457608 | tf_op jit(solution)/shard_map/ppermute | solution.py:172
  49.0 8.8 %collective-permute-done.1.rest_2_ = bf16[8,40,1280]{2,1,0:T(8,128)(2,1)} collective-permute-done((bf16[8,40,1280]{2,1,0:T(8,128)(2,1)S(1)}, bf16[8,40,1280]{2,1,0:T(8,128)(2,1)}, u32[]{:S(2)}, u32[]{:S(2)}) %collective-permute-start.1) | collective-permute-done | bytes 819232 | tf_op jit(solution)/shard_map/ppermute | solution.py:172
  57.8 3.2 %collective-permute-start.2 = (bf16[8,40,1280]{2,1,0:T(8,128)(2,1)}, bf16[8,40,1280]{2,1,0:T(8,128)(2,1)}, u32[]{:S(2)}, u32[]{:S(2)}) collective-permute-start(bf16[8,40,1280]{2,1,0:T(8,128)(2,1)} %collective-permute-done.1.rest_2_), channel_id=1, source_target_pairs={{0,384},{128,0},{256,128},{384,256},{1,385},{129,1},{257,129},{385... | collective-permute-start | bytes 2457608 | tf_op jit(solution)/shard_map/ppermute | solution.py:172
  61.7 1.3 reshape.226
  63.0 7.9 %all-to-all-start = ((bf16[64,2,1920]{2,1,0:T(2,128)(2,1)}), bf16[64,2,1920]{2,1,0:T(2,128)(2,1)S(1)}, u32[]{:S(2)}, u32[]{:S(2)}) async-start(bf16[64,2,1920]{2,1,0:T(2,128)(2,1)} %reshape.226), calls=%async_computation | async-start | bytes 983040 | tf_op jit(solution)/shard_map/all_to_all | solution.py:168
  71.0 2.0 %collective-permute-start.3 = (bf16[8,40,1280]{2,1,0:T(8,128)(2,1)S(1)}, bf16[8,40,1280]{2,1,0:T(8,128)(2,1)}, u32[]{:S(2)}, u32[]{:S(2)}) collective-permute-start(bf16[8,40,1280]{2,1,0:T(8,128)(2,1)S(1)} %all_to_all.25.rest_0_), channel_id=1, source_target_pairs={{0,8},{8,0},{1,9},{9,1},{2,10},{10,2},{3,11},{11,3},{4,12},{12,4},... | collective-permute-start | bytes 2457608 | tf_op jit(solution)/shard_map/ppermute | solution.py:172
  73.0 2.3 %collective-permute-start.5 = (bf16[8,40,1280]{2,1,0:T(8,128)(2,1)}, bf16[8,40,1280]{2,1,0:T(8,128)(2,1)}, u32[]{:S(2)}, u32[]{:S(2)}) collective-permute-start(bf16[8,40,1280]{2,1,0:T(8,128)(2,1)} %collective-permute-done.1.rest_2_), channel_id=1, source_target_pairs={{0,8},{8,0},{1,9},{9,1},{2,10},{10,2},{3,11},{11,3},{4,12},{12,4},... | collective-permute-start | bytes 2457608 | tf_op jit(solution)/shard_map/ppermute | solution.py:172
  75.3 2.0 %collective-permute-start.4 = (bf16[8,40,1280]{2,1,0:T(8,128)(2,1)}, bf16[8,40,1280]{2,1,0:T(8,128)(2,1)}, u32[]{:S(2)}, u32[]{:S(2)}) collective-permute-start(bf16[8,40,1280]{2,1,0:T(8,128)(2,1)} %collective-permute-done.rest_1_), channel_id=1, source_target_pairs={{0,8},{8,0},{1,9},{9,1},{2,10},{10,2},{3,11},{11,3},{4,12},{12,4},... | collective-permute-start | bytes 2457608 | tf_op jit(solution)/shard_map/ppermute | solution.py:172
  77.4 2.3 %collective-permute-start.6 = (bf16[8,40,1280]{2,1,0:T(8,128)(2,1)}, bf16[8,40,1280]{2,1,0:T(8,128)(2,1)}, u32[]{:S(2)}, u32[]{:S(2)}) collective-permute-start(bf16[8,40,1280]{2,1,0:T(8,128)(2,1)} %collective-permute-done.2.rest_3_), channel_id=1, source_target_pairs={{0,8},{8,0},{1,9},{9,1},{2,10},{10,2},{3,11},{11,3},{4,12},{12,4},... | collective-permute-start | bytes 2457608 | tf_op jit(solution)/shard_map/ppermute | solution.py:172
  80.1 1.1 reshape.229.grad_ref
  81.2 2.2 %collective-permute-start.8 = (bf16[192,1280]{1,0:T(8,128)(2,1)}, bf16[192,1280]{1,0:T(8,128)(2,1)S(1)}, u32[]{:S(2)}, u32[]{:S(2)}) collective-permute-start(bf16[192,1280]{1,0:T(8,128)(2,1)} %reshape.229.grad_ref), channel_id=1, source_target_pairs={{0,8},{8,0},{1,9},{9,1},{2,10},{10,2},{3,11},{11,3},{4,12},{12,4},... | collective-permute-start | bytes 1474568 | tf_op jit(solution)/shard_map/ppermute | solution.py:172
  83.4 1.3 dynamic-slice_bitcast_fusion
  84.6 0.8 copy.38.row_ref
  86.0 1.2 add_convert_fusion.pick_ref
  87.2 1.1 reshape.227.normed_ref
  88.3 13.4 %shard_map.103 = (bf16[192,1920]{1,0:T(8,128)(2,1)}, bf16[192,320]{1,0:T(8,128)(2,1)}, bf16[192,320]{1,0:T(8,128)(2,1)}, bf16[640,1280]{1,0:T(8,128)(2,1)}) custom-call(s32[2]{0:T(128)} %pad_add_fusion.place_ref, bf16[192,1280]{1,0:T(8,128)(2,1)} %reshape.227.normed_ref, bf16[192,1280]{1,0:T(8,128)(2,1)} %reshape.229.grad_ref, s32[192,1]{1,0:T(8,128)} %copy.38.row_ref, ...), custom_call_target="tpu_custom_call" | custom-call | tf_op jit(solution)/shard_map/pallas_call | solution.py:87
  101.7 3.4 %reshape.230 = bf16[64,2,2880]{2,1,0:T(2,128)(2,1)} reshape(bf16[192,1920]{1,0:T(8,128)(2,1)} %get-tuple-element.20) | data formatting | bytes 1474560 | tf_op jit(solution)/shard_map/reshape | solution.py:233
  105.1 13.8 %all-to-all-start.3 = ((bf16[64,2,2880]{2,1,0:T(2,128)(2,1)}), bf16[64,2,2880]{2,1,0:T(2,128)(2,1)S(1)}, u32[]{:S(2)}, u32[]{:S(2)}) async-start(bf16[64,2,2880]{2,1,0:T(2,128)(2,1)} %reshape.230), calls=%async_computation.3 | async-start | bytes 1507328 | tf_op jit(solution)/shard_map/all_to_all | solution.py:168
  118.9 2.0 %collective-permute-start.7 = (bf16[192,320]{1,0:T(8,128)(2,1)S(1)}, bf16[192,320]{1,0:T(8,128)(2,1)S(1)}, u32[]{:S(2)}, u32[]{:S(2)}) collective-permute-start(bf16[192,320]{1,0:T(8,128)(2,1)S(1)} %copy-done.7), channel_id=1, source_target_pairs={{0,8},{8,0},{1,9},{9,1},{2,10},{10,2},{3,11},{11,3},{4,12},{12,4},... | collective-permute-start | bytes 368648 | tf_op jit(solution)/shard_map/ppermute | solution.py:172
  120.9 1.2 collective-permute-done.7.got_ref
  122.1 1.8 shard_map.104
  123.9 4.2 %collective-permute-start.10 = (bf16[80,1280]{1,0:T(8,128)(2,1)S(1)}, bf16[80,1280]{1,0:T(8,128)(2,1)S(1)}, u32[]{:S(2)}, u32[]{:S(2)}) collective-permute-start(bf16[80,1280]{1,0:T(8,128)(2,1)S(1)} %get-tuple-element.26), channel_id=1, source_target_pairs={{0,256},{128,384},{256,0},{384,128},{1,257},{129,385},{257,1},{385... | collective-permute-start | bytes 614408 | tf_op jit(solution)/shard_map/ppermute | solution.py:172
  128.1 3.3 %collective-permute-start.11 = (bf16[80,1280]{1,0:T(8,128)(2,1)S(1)}, bf16[80,1280]{1,0:T(8,128)(2,1)S(1)}, u32[]{:S(2)}, u32[]{:S(2)}) collective-permute-start(bf16[80,1280]{1,0:T(8,128)(2,1)S(1)} %get-tuple-element.27), channel_id=1, source_target_pairs={{0,384},{128,0},{256,128},{384,256},{1,385},{129,1},{257,129},{385... | collective-permute-start | bytes 614408 | tf_op jit(solution)/shard_map/ppermute | solution.py:172
  131.4 2.6 %collective-permute-start.9 = (bf16[80,1280]{1,0:T(8,128)(2,1)S(1)}, bf16[80,1280]{1,0:T(8,128)(2,1)S(1)}, u32[]{:S(2)}, u32[]{:S(2)}) collective-permute-start(bf16[80,1280]{1,0:T(8,128)(2,1)S(1)} %get-tuple-element.25), channel_id=1, source_target_pairs={{0,128},{128,256},{256,384},{384,0},{1,129},{129,257},{257,385},{3... | collective-permute-start | bytes 614408 | tf_op jit(solution)/shard_map/ppermute | solution.py:172
  134.0 5.3 %collective-permute-done.10.rest_1_ = bf16[80,1280]{1,0:T(8,128)(2,1)S(1)} collective-permute-done((bf16[80,1280]{1,0:T(8,128)(2,1)S(1)}, bf16[80,1280]{1,0:T(8,128)(2,1)S(1)}, u32[]{:S(2)}, u32[]{:S(2)}) %collective-permute-start.10) | collective-permute-done | bytes 204832 | tf_op jit(solution)/shard_map/ppermute | solution.py:172
  139.3 4.2 %collective-permute-done.11.rest_2_ = bf16[80,1280]{1,0:T(8,128)(2,1)S(1)} collective-permute-done((bf16[80,1280]{1,0:T(8,128)(2,1)S(1)}, bf16[80,1280]{1,0:T(8,128)(2,1)S(1)}, u32[]{:S(2)}, u32[]{:S(2)}) %collective-permute-start.11) | collective-permute-done | bytes 204832 | tf_op jit(solution)/shard_map/ppermute | solution.py:172
  143.7 2.8 %collective-permute-start.12 = (bf16[10,1280]{1,0:T(8,128)(2,1)S(1)}, bf16[10,1280]{1,0:T(8,128)(2,1)S(1)}, u32[]{:S(2)}, u32[]{:S(2)}) collective-permute-start(bf16[10,1280]{1,0:T(8,128)(2,1)S(1)} %get-tuple-element.29), channel_id=1, source_target_pairs={{0,16},{16,32},{32,48},{48,64},{64,80},{80,96},{96,112},{112,0},{1... | collective-permute-start | bytes 76808 | tf_op jit(solution)/shard_map/ppermute | solution.py:172
  146.4 4.5 %collective-permute-start.13 = (bf16[10,1280]{1,0:T(8,128)(2,1)S(1)}, bf16[10,1280]{1,0:T(8,128)(2,1)S(1)}, u32[]{:S(2)}, u32[]{:S(2)}) collective-permute-start(bf16[10,1280]{1,0:T(8,128)(2,1)S(1)} %get-tuple-element.30), channel_id=1, source_target_pairs={{0,32},{16,48},{32,64},{48,80},{64,96},{80,112},{96,0},{112,16},{1... | collective-permute-start | bytes 76808 | tf_op jit(solution)/shard_map/ppermute | solution.py:172
  151.0 4.5 %collective-permute-start.14 = (bf16[10,1280]{1,0:T(8,128)(2,1)S(1)}, bf16[10,1280]{1,0:T(8,128)(2,1)S(1)}, u32[]{:S(2)}, u32[]{:S(2)}) collective-permute-start(bf16[10,1280]{1,0:T(8,128)(2,1)S(1)} %get-tuple-element.31), channel_id=1, source_target_pairs={{0,48},{16,64},{32,80},{48,96},{64,112},{80,0},{96,16},{112,32},{1... | collective-permute-start | bytes 76808 | tf_op jit(solution)/shard_map/ppermute | solution.py:172
  155.5 3.9 %collective-permute-start.15 = (bf16[10,1280]{1,0:T(8,128)(2,1)S(1)}, bf16[10,1280]{1,0:T(8,128)(2,1)S(1)}, u32[]{:S(2)}, u32[]{:S(2)}) collective-permute-start(bf16[10,1280]{1,0:T(8,128)(2,1)S(1)} %get-tuple-element.32), channel_id=1, source_target_pairs={{0,64},{16,80},{32,96},{48,112},{64,0},{80,16},{96,32},{112,48},{1... | collective-permute-start | bytes 76808 | tf_op jit(solution)/shard_map/ppermute | solution.py:172
  159.3 4.7 %collective-permute-start.16 = (bf16[10,1280]{1,0:T(8,128)(2,1)S(1)}, bf16[10,1280]{1,0:T(8,128)(2,1)S(1)}, u32[]{:S(2)}, u32[]{:S(2)}) collective-permute-start(bf16[10,1280]{1,0:T(8,128)(2,1)S(1)} %get-tuple-element.33), channel_id=1, source_target_pairs={{0,80},{16,96},{32,112},{48,0},{64,16},{80,32},{96,48},{112,64},{1... | collective-permute-start | bytes 76808 | tf_op jit(solution)/shard_map/ppermute | solution.py:172
  164.1 6.0 %collective-permute-start.17 = (bf16[10,1280]{1,0:T(8,128)(2,1)S(1)}, bf16[10,1280]{1,0:T(8,128)(2,1)S(1)}, u32[]{:S(2)}, u32[]{:S(2)}) collective-permute-start(bf16[10,1280]{1,0:T(8,128)(2,1)S(1)} %get-tuple-element.34), channel_id=1, source_target_pairs={{0,96},{16,112},{32,0},{48,16},{64,32},{80,48},{96,64},{112,80},{1... | collective-permute-start | bytes 76808 | tf_op jit(solution)/shard_map/ppermute | solution.py:172
  170.1 3.5 %collective-permute-start.18 = (bf16[10,1280]{1,0:T(8,128)(2,1)S(1)}, bf16[10,1280]{1,0:T(8,128)(2,1)S(1)}, u32[]{:S(2)}, u32[]{:S(2)}) collective-permute-start(bf16[10,1280]{1,0:T(8,128)(2,1)S(1)} %get-tuple-element.35), channel_id=1, source_target_pairs={{0,112},{16,0},{32,16},{48,32},{64,48},{80,64},{96,80},{112,96},{1... | collective-permute-start | bytes 76808 | tf_op jit(solution)/shard_map/ppermute | solution.py:172
  174.2 1.8 collective-permute-done.18
  176.1 0.8 broadcast_in_dim.11
  176.9 10.2 %all-to-all-start.4 = ((bf16[8,2,6400]{2,1,0:T(2,128)(2,1)}), bf16[8,2,6400]{2,1,0:T(2,128)(2,1)S(1)}, u32[]{:S(2)}, u32[]{:S(2)}) async-start(bf16[8,2,6400]{2,1,0:T(2,128)(2,1)} %broadcast_in_dim.11), calls=%async_computation.4 | async-start | bytes 409600 | tf_op jit(solution)/shard_map/all_to_all | solution.py:168
  187.1 1.1 reshape.231
  188.2 1.0 fusion.1
  189.2 2.0 %fusion.6 = bf16[1,3,64,1280]{3,1,2,0:T(4,128)(2,1)S(1)} fusion(f32[3,64]{0,1:T(8,128)S(1)} %broadcast_multiply_fusion, f32[3,64]{0,1:T(8,128)S(1)} %broadcast_multiply_fusion.2, f32[3,64]{0,1:T(8,128)S(1)} %broadcast_multiply_fusion.1, f32[1280]{0:T(1024)S(1)} %copy-done.6, f32[3,64]{0,1:T(8,128)S(1)} %add_rsqrt_fusion, ...), kind=kLoop, calls=%fused_computation.16 | loop fusion | flops 2949120 | bytes 1974272 | tf_op jit(solution)/shard_map/broadcast_in_dim | solution.py:257
  191.4 0.8 copy.41
  192.9 1.3 fusion
  194.2 2.7 %all-to-all-done.4 = bf16[8,2,6400]{2,1,0:T(2,128)(2,1)S(1)} async-done(((bf16[8,2,6400]{2,1,0:T(2,128)(2,1)}), bf16[8,2,6400]{2,1,0:T(2,128)(2,1)S(1)}, u32[]{:S(2)}, u32[]{:S(2)}) %all-to-all-start.4) | async-done | bytes 204832 | tf_op jit(solution)/shard_map/all_to_all | solution.py:168
  (55 shorter events, 5.8 us)
Async XLA Ops:
  2.2 33.4 %copy-start.3 = (bf16[1,3,64,1280]{3,2,1,0:T(8,128)(2,1)S(1)}, bf16[1,3,64,1280]{3,2,1,0:T(8,128)(2,1)}, u32[]{:S(2)}) copy-start(bf16[1,3,64,1280]{3,2,1,0:T(8,128)(2,1)} %param.10) | copy-start | bytes 1474564
  33.1 37.9 %copy-start.2 = (bf16[8,40,1280]{2,1,0:T(8,128)(2,1)}, bf16[8,40,1280]{2,1,0:T(8,128)(2,1)S(1)}, u32[]{:S(2)}) copy-start(bf16[8,40,1280]{2,1,0:T(8,128)(2,1)S(1)} %all_to_all.25.rest_0_) | copy-start | bytes 2457604
  33.1 24.7 %collective-permute-start.1 = (bf16[8,40,1280]{2,1,0:T(8,128)(2,1)S(1)}, bf16[8,40,1280]{2,1,0:T(8,128)(2,1)}, u32[]{:S(2)}, u32[]{:S(2)}) collective-permute-start(bf16[8,40,1280]{2,1,0:T(8,128)(2,1)S(1)} %all_to_all.25.rest_0_), channel_id=1, source_target_pairs={{0,384},{128,0},{256,128},{384,256},{1,385},{129,1},{257,129},{385... | collective-permute-start | bytes 2457608 | tf_op jit(solution)/shard_map/ppermute | solution.py:172
  36.0 8.4 %copy-start.1 = (bf16[1,3,64,1280]{3,2,1,0:T(8,128)(2,1)S(1)}, bf16[1,3,64,1280]{3,2,1,0:T(8,128)(2,1)}, u32[]{:S(2)}) copy-start(bf16[1,3,64,1280]{3,2,1,0:T(8,128)(2,1)} %param.8) | copy-start | bytes 1474564
  37.4 23.7 %copy-start.6 = (f32[1280]{0:T(1024)S(1)}, f32[1280]{0:T(1024)}, u32[]{:S(2)}) copy-start(f32[1280]{0:T(1024)} %param.11) | copy-start | bytes 15364
  37.4 25.7 %all-to-all-start.1 = ((bf16[64,2,1920]{2,1,0:T(2,128)(2,1)}), bf16[64,2,1920]{2,1,0:T(2,128)(2,1)S(1)}, u32[]{:S(2)}, u32[]{:S(2)}) async-start(bf16[64,2,1920]{2,1,0:T(2,128)(2,1)} %reshape.228), calls=%async_computation.1 | async-start | bytes 983040 | tf_op jit(solution)/shard_map/all_to_all | solution.py:168
  45.5 29.8 %collective-permute-start = (bf16[8,40,1280]{2,1,0:T(8,128)(2,1)S(1)}, bf16[8,40,1280]{2,1,0:T(8,128)(2,1)}, u32[]{:S(2)}, u32[]{:S(2)}) collective-permute-start(bf16[8,40,1280]{2,1,0:T(8,128)(2,1)S(1)} %all_to_all.25.rest_0_), channel_id=1, source_target_pairs={{0,128},{128,256},{256,384},{384,0},{1,129},{129,257},{257,385},{3... | collective-permute-start | bytes 2457608 | tf_op jit(solution)/shard_map/ppermute | solution.py:172
  57.8 19.6 %collective-permute-start.2 = (bf16[8,40,1280]{2,1,0:T(8,128)(2,1)}, bf16[8,40,1280]{2,1,0:T(8,128)(2,1)}, u32[]{:S(2)}, u32[]{:S(2)}) collective-permute-start(bf16[8,40,1280]{2,1,0:T(8,128)(2,1)} %collective-permute-done.1.rest_2_), channel_id=1, source_target_pairs={{0,384},{128,0},{256,128},{384,256},{1,385},{129,1},{257,129},{385... | collective-permute-start | bytes 2457608 | tf_op jit(solution)/shard_map/ppermute | solution.py:172
  63.0 24.2 %all-to-all-start = ((bf16[64,2,1920]{2,1,0:T(2,128)(2,1)}), bf16[64,2,1920]{2,1,0:T(2,128)(2,1)S(1)}, u32[]{:S(2)}, u32[]{:S(2)}) async-start(bf16[64,2,1920]{2,1,0:T(2,128)(2,1)} %reshape.226), calls=%async_computation | async-start | bytes 983040 | tf_op jit(solution)/shard_map/all_to_all | solution.py:168
  71.0 17.3 %collective-permute-start.3 = (bf16[8,40,1280]{2,1,0:T(8,128)(2,1)S(1)}, bf16[8,40,1280]{2,1,0:T(8,128)(2,1)}, u32[]{:S(2)}, u32[]{:S(2)}) collective-permute-start(bf16[8,40,1280]{2,1,0:T(8,128)(2,1)S(1)} %all_to_all.25.rest_0_), channel_id=1, source_target_pairs={{0,8},{8,0},{1,9},{9,1},{2,10},{10,2},{3,11},{11,3},{4,12},{12,4},... | collective-permute-start | bytes 2457608 | tf_op jit(solution)/shard_map/ppermute | solution.py:172
  73.0 15.2 %collective-permute-start.5 = (bf16[8,40,1280]{2,1,0:T(8,128)(2,1)}, bf16[8,40,1280]{2,1,0:T(8,128)(2,1)}, u32[]{:S(2)}, u32[]{:S(2)}) collective-permute-start(bf16[8,40,1280]{2,1,0:T(8,128)(2,1)} %collective-permute-done.1.rest_2_), channel_id=1, source_target_pairs={{0,8},{8,0},{1,9},{9,1},{2,10},{10,2},{3,11},{11,3},{4,12},{12,4},... | collective-permute-start | bytes 2457608 | tf_op jit(solution)/shard_map/ppermute | solution.py:172
  75.3 12.9 %collective-permute-start.4 = (bf16[8,40,1280]{2,1,0:T(8,128)(2,1)}, bf16[8,40,1280]{2,1,0:T(8,128)(2,1)}, u32[]{:S(2)}, u32[]{:S(2)}) collective-permute-start(bf16[8,40,1280]{2,1,0:T(8,128)(2,1)} %collective-permute-done.rest_1_), channel_id=1, source_target_pairs={{0,8},{8,0},{1,9},{9,1},{2,10},{10,2},{3,11},{11,3},{4,12},{12,4},... | collective-permute-start | bytes 2457608 | tf_op jit(solution)/shard_map/ppermute | solution.py:172
  77.4 10.9 %collective-permute-start.6 = (bf16[8,40,1280]{2,1,0:T(8,128)(2,1)}, bf16[8,40,1280]{2,1,0:T(8,128)(2,1)}, u32[]{:S(2)}, u32[]{:S(2)}) collective-permute-start(bf16[8,40,1280]{2,1,0:T(8,128)(2,1)} %collective-permute-done.2.rest_3_), channel_id=1, source_target_pairs={{0,8},{8,0},{1,9},{9,1},{2,10},{10,2},{3,11},{11,3},{4,12},{12,4},... | collective-permute-start | bytes 2457608 | tf_op jit(solution)/shard_map/ppermute | solution.py:172
  81.2 39.7 %collective-permute-start.8 = (bf16[192,1280]{1,0:T(8,128)(2,1)}, bf16[192,1280]{1,0:T(8,128)(2,1)S(1)}, u32[]{:S(2)}, u32[]{:S(2)}) collective-permute-start(bf16[192,1280]{1,0:T(8,128)(2,1)} %reshape.229.grad_ref), channel_id=1, source_target_pairs={{0,8},{8,0},{1,9},{9,1},{2,10},{10,2},{3,11},{11,3},{4,12},{12,4},... | collective-permute-start | bytes 1474568 | tf_op jit(solution)/shard_map/ppermute | solution.py:172
  101.7 17.2 %copy-start.7 = (bf16[192,320]{1,0:T(8,128)(2,1)S(1)}, bf16[192,320]{1,0:T(8,128)(2,1)}, u32[]{:S(2)}) copy-start(bf16[192,320]{1,0:T(8,128)(2,1)} %get-tuple-element.23) | copy-start | bytes 368644
  101.7 20.4 %copy-start = (bf16[192,320]{1,0:T(8,128)(2,1)S(1)}, bf16[192,320]{1,0:T(8,128)(2,1)}, u32[]{:S(2)}) copy-start(bf16[192,320]{1,0:T(8,128)(2,1)} %get-tuple-element.22.own_ref) | copy-start | bytes 368644
  105.1 71.0 %all-to-all-start.3 = ((bf16[64,2,2880]{2,1,0:T(2,128)(2,1)}), bf16[64,2,2880]{2,1,0:T(2,128)(2,1)S(1)}, u32[]{:S(2)}, u32[]{:S(2)}) async-start(bf16[64,2,2880]{2,1,0:T(2,128)(2,1)} %reshape.230), calls=%async_computation.3 | async-start | bytes 1507328 | tf_op jit(solution)/shard_map/all_to_all | solution.py:168
  118.9 3.3 %collective-permute-start.7 = (bf16[192,320]{1,0:T(8,128)(2,1)S(1)}, bf16[192,320]{1,0:T(8,128)(2,1)S(1)}, u32[]{:S(2)}, u32[]{:S(2)}) collective-permute-start(bf16[192,320]{1,0:T(8,128)(2,1)S(1)} %copy-done.7), channel_id=1, source_target_pairs={{0,8},{8,0},{1,9},{9,1},{2,10},{10,2},{3,11},{11,3},{4,12},{12,4},... | collective-permute-start | bytes 368648 | tf_op jit(solution)/shard_map/ppermute | solution.py:172
  123.9 15.3 %collective-permute-start.10 = (bf16[80,1280]{1,0:T(8,128)(2,1)S(1)}, bf16[80,1280]{1,0:T(8,128)(2,1)S(1)}, u32[]{:S(2)}, u32[]{:S(2)}) collective-permute-start(bf16[80,1280]{1,0:T(8,128)(2,1)S(1)} %get-tuple-element.26), channel_id=1, source_target_pairs={{0,256},{128,384},{256,0},{384,128},{1,257},{129,385},{257,1},{385... | collective-permute-start | bytes 614408 | tf_op jit(solution)/shard_map/ppermute | solution.py:172
  128.1 15.3 %collective-permute-start.11 = (bf16[80,1280]{1,0:T(8,128)(2,1)S(1)}, bf16[80,1280]{1,0:T(8,128)(2,1)S(1)}, u32[]{:S(2)}, u32[]{:S(2)}) collective-permute-start(bf16[80,1280]{1,0:T(8,128)(2,1)S(1)} %get-tuple-element.27), channel_id=1, source_target_pairs={{0,384},{128,0},{256,128},{384,256},{1,385},{129,1},{257,129},{385... | collective-permute-start | bytes 614408 | tf_op jit(solution)/shard_map/ppermute | solution.py:172
  131.4 12.1 %collective-permute-start.9 = (bf16[80,1280]{1,0:T(8,128)(2,1)S(1)}, bf16[80,1280]{1,0:T(8,128)(2,1)S(1)}, u32[]{:S(2)}, u32[]{:S(2)}) collective-permute-start(bf16[80,1280]{1,0:T(8,128)(2,1)S(1)} %get-tuple-element.25), channel_id=1, source_target_pairs={{0,128},{128,256},{256,384},{384,0},{1,129},{129,257},{257,385},{3... | collective-permute-start | bytes 614408 | tf_op jit(solution)/shard_map/ppermute | solution.py:172
  143.7 20.4 %collective-permute-start.12 = (bf16[10,1280]{1,0:T(8,128)(2,1)S(1)}, bf16[10,1280]{1,0:T(8,128)(2,1)S(1)}, u32[]{:S(2)}, u32[]{:S(2)}) collective-permute-start(bf16[10,1280]{1,0:T(8,128)(2,1)S(1)} %get-tuple-element.29), channel_id=1, source_target_pairs={{0,16},{16,32},{32,48},{48,64},{64,80},{80,96},{96,112},{112,0},{1... | collective-permute-start | bytes 76808 | tf_op jit(solution)/shard_map/ppermute | solution.py:172
  146.4 23.7 %collective-permute-start.13 = (bf16[10,1280]{1,0:T(8,128)(2,1)S(1)}, bf16[10,1280]{1,0:T(8,128)(2,1)S(1)}, u32[]{:S(2)}, u32[]{:S(2)}) collective-permute-start(bf16[10,1280]{1,0:T(8,128)(2,1)S(1)} %get-tuple-element.30), channel_id=1, source_target_pairs={{0,32},{16,48},{32,64},{48,80},{64,96},{80,112},{96,0},{112,16},{1... | collective-permute-start | bytes 76808 | tf_op jit(solution)/shard_map/ppermute | solution.py:172
  151.0 23.2 %collective-permute-start.14 = (bf16[10,1280]{1,0:T(8,128)(2,1)S(1)}, bf16[10,1280]{1,0:T(8,128)(2,1)S(1)}, u32[]{:S(2)}, u32[]{:S(2)}) collective-permute-start(bf16[10,1280]{1,0:T(8,128)(2,1)S(1)} %get-tuple-element.31), channel_id=1, source_target_pairs={{0,48},{16,64},{32,80},{48,96},{64,112},{80,0},{96,16},{112,32},{1... | collective-permute-start | bytes 76808 | tf_op jit(solution)/shard_map/ppermute | solution.py:172
  155.5 18.8 %collective-permute-start.15 = (bf16[10,1280]{1,0:T(8,128)(2,1)S(1)}, bf16[10,1280]{1,0:T(8,128)(2,1)S(1)}, u32[]{:S(2)}, u32[]{:S(2)}) collective-permute-start(bf16[10,1280]{1,0:T(8,128)(2,1)S(1)} %get-tuple-element.32), channel_id=1, source_target_pairs={{0,64},{16,80},{32,96},{48,112},{64,0},{80,16},{96,32},{112,48},{1... | collective-permute-start | bytes 76808 | tf_op jit(solution)/shard_map/ppermute | solution.py:172
  159.3 14.9 %collective-permute-start.16 = (bf16[10,1280]{1,0:T(8,128)(2,1)S(1)}, bf16[10,1280]{1,0:T(8,128)(2,1)S(1)}, u32[]{:S(2)}, u32[]{:S(2)}) collective-permute-start(bf16[10,1280]{1,0:T(8,128)(2,1)S(1)} %get-tuple-element.33), channel_id=1, source_target_pairs={{0,80},{16,96},{32,112},{48,0},{64,16},{80,32},{96,48},{112,64},{1... | collective-permute-start | bytes 76808 | tf_op jit(solution)/shard_map/ppermute | solution.py:172
  164.1 10.2 %collective-permute-start.17 = (bf16[10,1280]{1,0:T(8,128)(2,1)S(1)}, bf16[10,1280]{1,0:T(8,128)(2,1)S(1)}, u32[]{:S(2)}, u32[]{:S(2)}) collective-permute-start(bf16[10,1280]{1,0:T(8,128)(2,1)S(1)} %get-tuple-element.34), channel_id=1, source_target_pairs={{0,96},{16,112},{32,0},{48,16},{64,32},{80,48},{96,64},{112,80},{1... | collective-permute-start | bytes 76808 | tf_op jit(solution)/shard_map/ppermute | solution.py:172
  170.1 5.9 %collective-permute-start.18 = (bf16[10,1280]{1,0:T(8,128)(2,1)S(1)}, bf16[10,1280]{1,0:T(8,128)(2,1)S(1)}, u32[]{:S(2)}, u32[]{:S(2)}) collective-permute-start(bf16[10,1280]{1,0:T(8,128)(2,1)S(1)} %get-tuple-element.35), channel_id=1, source_target_pairs={{0,112},{16,0},{32,16},{48,32},{64,48},{80,64},{96,80},{112,96},{1... | collective-permute-start | bytes 76808 | tf_op jit(solution)/shard_map/ppermute | solution.py:172
  176.9 20.0 %all-to-all-start.4 = ((bf16[8,2,6400]{2,1,0:T(2,128)(2,1)}), bf16[8,2,6400]{2,1,0:T(2,128)(2,1)S(1)}, u32[]{:S(2)}, u32[]{:S(2)}) async-start(bf16[8,2,6400]{2,1,0:T(2,128)(2,1)} %broadcast_in_dim.11), calls=%async_computation.4 | async-start | bytes 409600 | tf_op jit(solution)/shard_map/all_to_all | solution.py:168
  188.2 1.1 copy-start.4
  191.3 1.6 copy-start.5

commit v2 on v0

--- a/solution.py
+++ b/solution.py
@@ -133,6 +133,34 @@
     )(place, own, got, grad, got_grad)
 
 
+def halve_kernel(bit_ref, stayed_ref, *rest):
+    came, stay_ref, send_ref = rest[:-2], rest[-2], rest[-1]
+    total = stayed_ref[...]
+    for piece in came:
+        total = total + piece[...].astype(jnp.float32)
+    rows = stay_ref.shape[0]
+    for side in range(2):
+        @pl.when(bit_ref[0] == side)
+        def _():
+            stay_ref[...] = total[side * rows:(side + 1) * rows]
+            send_ref[...] = total[(1 - side) * rows:(2 - side) * rows].astype(send_ref.dtype)
+
+
+def halve(bit, stayed, came, interpret=False):
+    rows, width = stayed.shape[0] // 2, stayed.shape[1]
+    return pl.pallas_call(
+        halve_kernel,
+        out_shape=(
+            jax.ShapeDtypeStruct((rows, width), jnp.float32),
+            jax.ShapeDtypeStruct((rows, width), jnp.bfloat16),
+        ),
+        in_specs=[pl.BlockSpec(memory_space=pltpu.SMEM)]
+        + [pl.BlockSpec(memory_space=pltpu.VMEM)] * (1 + len(came)),
+        compiler_params=pltpu.CompilerParams(vmem_limit_bytes=32 << 20),
+        interpret=interpret,
+    )(bit, stayed, *came)
+
+
 def exchange(values, axis):
     return lax.all_to_all(values, axis, split_axis=0, concat_axis=0, tiled=True)
 
@@ -186,6 +214,7 @@
     per = att // shards
     column = jnp.arange(att, dtype=jnp.int32)
     x, y = column // (per * 16), column // (per * 2) % 8
+    y = y % 2 * 4 + y // 2 % 2 * 2 + y // 4
     place = (x * 8 + y) * per + column % per
     side = column // per % 2
     at = place[:, None] == jnp.arange(att // 2, dtype=jnp.int32)[None, :]
@@ -205,12 +234,15 @@
     slabs = weight_part(
         lax.axis_index("x").astype(jnp.int32)[None], own, got, grad_cells, grad_got
     )
-    part = slabs[0]
-    for k in range(1, SIZES[0]):
-        part = part + shift(slabs[k], "x", k, SIZES[0]).astype(jnp.float32)
-    part = part.astype(low).reshape(SIZES[1], 2, -1)
-    part, _ = lax.optimization_barrier((part, back))
-    part = jnp.sum(exchange(part, "y").astype(jnp.float32), axis=0).astype(low)
+    came = [shift(slabs[k], "x", k, SIZES[0]) for k in range(1, SIZES[0])]
+    stay = slabs[0]
+    for level in range(3):
+        bit = ((lax.axis_index("y") >> level) & 1).astype(jnp.int32)[None]
+        stay, send = halve(bit, stay, came)
+        flips = [(i, i ^ (1 << level)) for i in range(SIZES[1])]
+        came = [lax.ppermute(send, "y", flips)]
+    part = stay + came[0].astype(jnp.float32)
+    part, _ = lax.optimization_barrier((part.astype(low).reshape(2, -1), back))
     part = exchange(jnp.broadcast_to(part[None], (clips,) + part.shape), "dp")
     grad_weight = jnp.sum(part.astype(jnp.float32), axis=0).reshape(per, width)
 

time: 185 us -> 192 us (1.038)
  starting transfers between devices: 77.3 us -> 85.3 us
  waiting for transfers between devices: 31.9 us -> 29.3 us
  local copies, waits for them, and re-layouts: 16.6 us -> 18.8 us
    ppermute x0 -> x3, starting transfers between devices: none -> 14.1 us  [on_device(): came = [lax.ppermute(send, 'y', flips)]]
    all_to_all x5 -> x4, waiting for transfers between devices: 13 us -> 0.64 us  [exchange(): return lax.all_to_all(values, axis, split_axis=0, concat_axis=0, tiled=True)]
    ppermute x0 -> x3, waiting for transfers between devices: none -> 9.36 us  [on_device(): came = [lax.ppermute(send, 'y', flips)]]
    all_to_all x5 -> x4, starting transfers between devices: 45.3 us -> 38.8 us  [exchange(): return lax.all_to_all(values, axis, split_axis=0, concat_axis=0, tiled=True)]
    reshape x1, local copies, waits for them, and re-layouts: 1.06 us -> 3.16 us  [on_device(): rows = back.reshape(shards, frames, att + width).transpose(1, 0, 2)]
  transfers between devices with their start and end apart: 17 -> 19, of which waited for: 6 -> 7; matrix products, arithmetic and copies ran while one was open for 13% -> 13% of each run, Pallas kernels for 8% -> 8%
where the time goes in v2:
time: 192 us; the launch traced here: 190 us
  starting transfers between devices  85.3 us (44%)
  blocking collectives  30.8 us (16%)
  waiting for transfers between devices  29.3 us (15%)
  local copies, waits for them, and re-layouts  18.8 us (10%)
  Pallas kernels  15.3 us (8%)
  other arithmetic  8.4 us (4%)
    all_to_all x4, starting transfers between devices, exchange(): return lax.all_to_all(values, axis, split_axis=0, concat_axis=0, tiled=True)  38.8 us
    ppermute x12, starting transfers between devices, shift(): lax.ppermute(values, axis, [(i, (i + step) % size) for i in range(size)])  32.3 us
    all_to_all x1, blocking collectives, exchange(): return lax.all_to_all(values, axis, split_axis=0, concat_axis=0, tiled=True)  30.8 us
    ppermute x12, waiting for transfers between devices, shift(): lax.ppermute(values, axis, [(i, (i + step) % size) for i in range(size)])  19.3 us
    ppermute x3, starting transfers between devices, on_device(): came = [lax.ppermute(send, 'y', flips)]  14.1 us
    pallas_call x1, Pallas kernels, cell_part(): pl.pallas_call(cell_kernel, out_shape=(jax.ShapeDtypeStruct((rows, att +...  13.4 us
    ppermute x3, waiting for transfers between devices, on_device(): came = [lax.ppermute(send, 'y', flips)]  9.36 us
  transfers between devices with their start and end apart: 19, of which 7 were waited for; matrix products, arithmetic and copies ran while one was open for 13% of the time, Pallas kernels for 8%

profile of v2, /device:TPU:2, one launch (start us, length us, event | category | flops | bytes accessed | tf_op | source)
XLA Modules:
  0.0 190.5 jit_solution(7480753272997301334)
XLA Ops:
  0.6 0.8 fusion.34
  1.4 0.8 maximum_maximum_fusion
  2.3 30.8 %all_to_all.25.rest_0_ = bf16[8,40,1280]{2,1,0:T(8,128)(2,1)S(1)} all-to-all(bf16[8,40,1280]{2,1,0:T(8,128)(2,1)S(1)} %broadcast_in_dim.12), channel_id=1, replica_groups=mesh['x'=4,'y'=8,'core'=2,'dp'=8] {'y'}, dimensions={0} | all-to-all | bytes 1638400 | tf_op jit(solution)/shard_map/all_to_all | solution.py:165
  33.1 2.4 %collective-permute-start.1 = (bf16[8,40,1280]{2,1,0:T(8,128)(2,1)S(1)}, bf16[8,40,1280]{2,1,0:T(8,128)(2,1)}, u32[]{:S(2)}, u32[]{:S(2)}) collective-permute-start(bf16[8,40,1280]{2,1,0:T(8,128)(2,1)S(1)} %all_to_all.25.rest_0_), channel_id=1, source_target_pairs={{0,384},{128,0},{256,128},{384,256},{1,385},{129,1},{257,129},{385... | collective-permute-start | bytes 2457608 | tf_op jit(solution)/shard_map/ppermute | solution.py:169
  36.0 1.3 reshape.279
  37.4 7.1 %all-to-all-start.1 = ((bf16[64,2,1920]{2,1,0:T(2,128)(2,1)}), bf16[64,2,1920]{2,1,0:T(2,128)(2,1)S(1)}, u32[]{:S(2)}, u32[]{:S(2)}) async-start(bf16[64,2,1920]{2,1,0:T(2,128)(2,1)} %reshape.279), calls=%async_computation.1 | async-start | bytes 983040 | tf_op jit(solution)/shard_map/all_to_all | solution.py:165
  44.9 0.6 multiply_reduce_fusion.1
  45.5 3.5 %collective-permute-start = (bf16[8,40,1280]{2,1,0:T(8,128)(2,1)S(1)}, bf16[8,40,1280]{2,1,0:T(8,128)(2,1)}, u32[]{:S(2)}, u32[]{:S(2)}) collective-permute-start(bf16[8,40,1280]{2,1,0:T(8,128)(2,1)S(1)} %all_to_all.25.rest_0_), channel_id=1, source_target_pairs={{0,128},{128,256},{256,384},{384,0},{1,129},{129,257},{257,385},{3... | collective-permute-start | bytes 2457608 | tf_op jit(solution)/shard_map/ppermute | solution.py:169
  49.0 8.8 %collective-permute-done.1.rest_2_ = bf16[8,40,1280]{2,1,0:T(8,128)(2,1)} collective-permute-done((bf16[8,40,1280]{2,1,0:T(8,128)(2,1)S(1)}, bf16[8,40,1280]{2,1,0:T(8,128)(2,1)}, u32[]{:S(2)}, u32[]{:S(2)}) %collective-permute-start.1) | collective-permute-done | bytes 819232 | tf_op jit(solution)/shard_map/ppermute | solution.py:169
  57.8 3.2 %collective-permute-start.2 = (bf16[8,40,1280]{2,1,0:T(8,128)(2,1)}, bf16[8,40,1280]{2,1,0:T(8,128)(2,1)}, u32[]{:S(2)}, u32[]{:S(2)}) collective-permute-start(bf16[8,40,1280]{2,1,0:T(8,128)(2,1)} %collective-permute-done.1.rest_2_), channel_id=1, source_target_pairs={{0,384},{128,0},{256,128},{384,256},{1,385},{129,1},{257,129},{385... | collective-permute-start | bytes 2457608 | tf_op jit(solution)/shard_map/ppermute | solution.py:169
  61.7 1.3 reshape.277
  63.0 7.9 %all-to-all-start = ((bf16[64,2,1920]{2,1,0:T(2,128)(2,1)}), bf16[64,2,1920]{2,1,0:T(2,128)(2,1)S(1)}, u32[]{:S(2)}, u32[]{:S(2)}) async-start(bf16[64,2,1920]{2,1,0:T(2,128)(2,1)} %reshape.277), calls=%async_computation | async-start | bytes 983040 | tf_op jit(solution)/shard_map/all_to_all | solution.py:165
  71.0 2.0 %collective-permute-start.3 = (bf16[8,40,1280]{2,1,0:T(8,128)(2,1)S(1)}, bf16[8,40,1280]{2,1,0:T(8,128)(2,1)S(1)}, u32[]{:S(2)}, u32[]{:S(2)}) collective-permute-start(bf16[8,40,1280]{2,1,0:T(8,128)(2,1)S(1)} %all_to_all.25.rest_0_), channel_id=1, source_target_pairs={{0,8},{8,0},{1,9},{9,1},{2,10},{10,2},{3,11},{11,3},{4,12},{12,4},... | collective-permute-start | bytes 2457608 | tf_op jit(solution)/shard_map/ppermute | solution.py:169
  73.0 2.3 %collective-permute-start.5 = (bf16[8,40,1280]{2,1,0:T(8,128)(2,1)}, bf16[8,40,1280]{2,1,0:T(8,128)(2,1)}, u32[]{:S(2)}, u32[]{:S(2)}) collective-permute-start(bf16[8,40,1280]{2,1,0:T(8,128)(2,1)} %collective-permute-done.1.rest_2_), channel_id=1, source_target_pairs={{0,8},{8,0},{1,9},{9,1},{2,10},{10,2},{3,11},{11,3},{4,12},{12,4},... | collective-permute-start | bytes 2457608 | tf_op jit(solution)/shard_map/ppermute | solution.py:169
  75.3 2.0 %collective-permute-start.4 = (bf16[8,40,1280]{2,1,0:T(8,128)(2,1)}, bf16[8,40,1280]{2,1,0:T(8,128)(2,1)}, u32[]{:S(2)}, u32[]{:S(2)}) collective-permute-start(bf16[8,40,1280]{2,1,0:T(8,128)(2,1)} %collective-permute-done.rest_1_), channel_id=1, source_target_pairs={{0,8},{8,0},{1,9},{9,1},{2,10},{10,2},{3,11},{11,3},{4,12},{12,4},... | collective-permute-start | bytes 2457608 | tf_op jit(solution)/shard_map/ppermute | solution.py:169
  77.4 2.3 %collective-permute-start.6 = (bf16[8,40,1280]{2,1,0:T(8,128)(2,1)}, bf16[8,40,1280]{2,1,0:T(8,128)(2,1)}, u32[]{:S(2)}, u32[]{:S(2)}) collective-permute-start(bf16[8,40,1280]{2,1,0:T(8,128)(2,1)} %collective-permute-done.2.rest_3_), channel_id=1, source_target_pairs={{0,8},{8,0},{1,9},{9,1},{2,10},{10,2},{3,11},{11,3},{4,12},{12,4},... | collective-permute-start | bytes 2457608 | tf_op jit(solution)/shard_map/ppermute | solution.py:169
  79.7 1.3 dynamic-slice_bitcast_fusion
  81.0 0.8 copy.38.row_ref
  81.7 0.7 pad_add_fusion.place_ref
  82.4 1.1 reshape.280.grad_ref
  83.5 2.2 %collective-permute-start.8 = (bf16[192,1280]{1,0:T(8,128)(2,1)}, bf16[192,1280]{1,0:T(8,128)(2,1)S(1)}, u32[]{:S(2)}, u32[]{:S(2)}) collective-permute-start(bf16[192,1280]{1,0:T(8,128)(2,1)} %reshape.280.grad_ref), channel_id=1, source_target_pairs={{0,8},{8,0},{1,9},{9,1},{2,10},{10,2},{3,11},{11,3},{4,12},{12,4},... | collective-permute-start | bytes 1474568 | tf_op jit(solution)/shard_map/ppermute | solution.py:169
  86.1 1.2 add_convert_fusion.pick_ref
  87.2 1.1 reshape.278.normed_ref
  88.4 0.9 copy-done.6
  89.2 13.4 %shard_map.103 = (bf16[192,1920]{1,0:T(8,128)(2,1)}, bf16[192,320]{1,0:T(8,128)(2,1)}, bf16[192,320]{1,0:T(8,128)(2,1)}, bf16[640,1280]{1,0:T(8,128)(2,1)}) custom-call(s32[2]{0:T(128)} %pad_add_fusion.place_ref, bf16[192,1280]{1,0:T(8,128)(2,1)} %reshape.278.normed_ref, bf16[192,1280]{1,0:T(8,128)(2,1)} %reshape.280.grad_ref, s32[192,1]{1,0:T(8,128)} %copy.38.row_ref, ...), custom_call_target="tpu_custom_call" | custom-call | tf_op jit(solution)/shard_map/pallas_call | solution.py:87
  102.6 2.3 %collective-permute-start.7 = (bf16[192,320]{1,0:T(8,128)(2,1)}, bf16[192,320]{1,0:T(8,128)(2,1)S(1)}, u32[]{:S(2)}, u32[]{:S(2)}) collective-permute-start(bf16[192,320]{1,0:T(8,128)(2,1)} %get-tuple-element.21), channel_id=1, source_target_pairs={{0,8},{8,0},{1,9},{9,1},{2,10},{10,2},{3,11},{11,3},{4,12},{12,4},... | collective-permute-start | bytes 368648 | tf_op jit(solution)/shard_map/ppermute | solution.py:169
  104.9 3.4 %reshape.281 = bf16[64,2,2880]{2,1,0:T(2,128)(2,1)} reshape(bf16[192,1920]{1,0:T(8,128)(2,1)} %get-tuple-element.18) | data formatting | bytes 1474560 | tf_op jit(solution)/shard_map/reshape | solution.py:230
  108.3 13.6 %all-to-all-start.3 = ((bf16[64,2,2880]{2,1,0:T(2,128)(2,1)}), bf16[64,2,2880]{2,1,0:T(2,128)(2,1)}, u32[]{:S(2)}, u32[]{:S(2)}) async-start(bf16[64,2,2880]{2,1,0:T(2,128)(2,1)} %reshape.281), calls=%async_computation.3 | async-start | bytes 1507328 | tf_op jit(solution)/shard_map/all_to_all | solution.py:165
  122.0 1.8 shard_map.104
  123.7 4.2 %collective-permute-start.10 = (bf16[80,1280]{1,0:T(8,128)(2,1)S(1)}, bf16[80,1280]{1,0:T(8,128)(2,1)S(1)}, u32[]{:S(2)}, u32[]{:S(2)}) collective-permute-start(bf16[80,1280]{1,0:T(8,128)(2,1)S(1)} %get-tuple-element.24), channel_id=1, source_target_pairs={{0,256},{128,384},{256,0},{384,128},{1,257},{129,385},{257,1},{385... | collective-permute-start | bytes 614408 | tf_op jit(solution)/shard_map/ppermute | solution.py:169
  127.9 3.3 %collective-permute-start.11 = (bf16[80,1280]{1,0:T(8,128)(2,1)S(1)}, bf16[80,1280]{1,0:T(8,128)(2,1)S(1)}, u32[]{:S(2)}, u32[]{:S(2)}) collective-permute-start(bf16[80,1280]{1,0:T(8,128)(2,1)S(1)} %get-tuple-element.25), channel_id=1, source_target_pairs={{0,384},{128,0},{256,128},{384,256},{1,385},{129,1},{257,129},{385... | collective-permute-start | bytes 614408 | tf_op jit(solution)/shard_map/ppermute | solution.py:169
  131.2 2.6 %collective-permute-start.9 = (bf16[80,1280]{1,0:T(8,128)(2,1)S(1)}, bf16[80,1280]{1,0:T(8,128)(2,1)S(1)}, u32[]{:S(2)}, u32[]{:S(2)}) collective-permute-start(bf16[80,1280]{1,0:T(8,128)(2,1)S(1)} %get-tuple-element.23), channel_id=1, source_target_pairs={{0,128},{128,256},{256,384},{384,0},{1,129},{129,257},{257,385},{3... | collective-permute-start | bytes 614408 | tf_op jit(solution)/shard_map/ppermute | solution.py:169
  133.8 4.7 %collective-permute-done.10.rest_1_ = bf16[80,1280]{1,0:T(8,128)(2,1)S(1)} collective-permute-done((bf16[80,1280]{1,0:T(8,128)(2,1)S(1)}, bf16[80,1280]{1,0:T(8,128)(2,1)S(1)}, u32[]{:S(2)}, u32[]{:S(2)}) %collective-permute-start.10) | collective-permute-done | bytes 204832 | tf_op jit(solution)/shard_map/ppermute | solution.py:169
  138.4 5.9 %collective-permute-done.11.rest_2_ = bf16[80,1280]{1,0:T(8,128)(2,1)S(1)} collective-permute-done((bf16[80,1280]{1,0:T(8,128)(2,1)S(1)}, bf16[80,1280]{1,0:T(8,128)(2,1)S(1)}, u32[]{:S(2)}, u32[]{:S(2)}) %collective-permute-start.11) | collective-permute-done | bytes 204832 | tf_op jit(solution)/shard_map/ppermute | solution.py:169
  144.5 2.9 %collective-permute-start.12 = (bf16[40,1280]{1,0:T(8,128)(2,1)S(1)}, bf16[40,1280]{1,0:T(8,128)(2,1)S(1)}, u32[]{:S(2)}, u32[]{:S(2)}) collective-permute-start(bf16[40,1280]{1,0:T(8,128)(2,1)S(1)} %get-tuple-element.27), channel_id=1, source_target_pairs={{0,16},{16,0},{32,48},{48,32},{64,80},{80,64},{96,112},{112,96},{1... | collective-permute-start | bytes 307208 | tf_op jit(solution)/shard_map/ppermute | solution.py:243
  147.4 3.8 %collective-permute-done.12.rest_0_ = bf16[40,1280]{1,0:T(8,128)(2,1)S(1)} collective-permute-done((bf16[40,1280]{1,0:T(8,128)(2,1)S(1)}, bf16[40,1280]{1,0:T(8,128)(2,1)S(1)}, u32[]{:S(2)}, u32[]{:S(2)}) %collective-permute-start.12) | collective-permute-done | bytes 102432 | tf_op jit(solution)/shard_map/ppermute | solution.py:243
  151.2 3.9 %collective-permute-start.13 = (bf16[20,1280]{1,0:T(8,128)(2,1)S(1)}, bf16[20,1280]{1,0:T(8,128)(2,1)S(1)}, u32[]{:S(2)}, u32[]{:S(2)}) collective-permute-start(bf16[20,1280]{1,0:T(8,128)(2,1)S(1)} %get-tuple-element.29), channel_id=1, source_target_pairs={{0,32},{16,48},{32,0},{48,16},{64,96},{80,112},{96,64},{112,80},{1... | collective-permute-start | bytes 153608 | tf_op jit(solution)/shard_map/ppermute | solution.py:243
  155.1 3.8 %collective-permute-done.13.rest_0_ = bf16[20,1280]{1,0:T(8,128)(2,1)S(1)} collective-permute-done((bf16[20,1280]{1,0:T(8,128)(2,1)S(1)}, bf16[20,1280]{1,0:T(8,128)(2,1)S(1)}, u32[]{:S(2)}, u32[]{:S(2)}) %collective-permute-start.13) | collective-permute-done | bytes 51232 | tf_op jit(solution)/shard_map/ppermute | solution.py:243
  158.9 7.4 %collective-permute-start.14 = (bf16[10,1280]{1,0:T(8,128)(2,1)S(1)}, bf16[10,1280]{1,0:T(8,128)(2,1)S(1)}, u32[]{:S(2)}, u32[]{:S(2)}) collective-permute-start(bf16[10,1280]{1,0:T(8,128)(2,1)S(1)} %get-tuple-element.31), channel_id=1, source_target_pairs={{0,64},{16,80},{32,96},{48,112},{64,0},{80,16},{96,32},{112,48},{1... | collective-permute-start | bytes 76808 | tf_op jit(solution)/shard_map/ppermute | solution.py:243
  166.9 1.8 collective-permute-done.14
  168.8 0.8 broadcast_in_dim.17
  169.6 10.2 %all-to-all-start.4 = ((bf16[8,2,6400]{2,1,0:T(2,128)(2,1)}), bf16[8,2,6400]{2,1,0:T(2,128)(2,1)S(1)}, u32[]{:S(2)}, u32[]{:S(2)}) async-start(bf16[8,2,6400]{2,1,0:T(2,128)(2,1)} %broadcast_in_dim.17), calls=%async_computation.4 | async-start | bytes 409600 | tf_op jit(solution)/shard_map/all_to_all | solution.py:165
  179.8 3.2 %reshape.282 = bf16[64,3,1920]{2,1,0:T(4,128)(2,1)S(1)} reshape(bf16[64,2,2880]{2,1,0:T(2,128)(2,1)} %all-to-all-done.3) | data formatting | bytes 1474560 | tf_op jit(solution)/shard_map/reshape | solution.py:231
  182.9 1.0 fusion.1
  184.0 2.0 %fusion.6 = bf16[1,3,64,1280]{3,1,2,0:T(4,128)(2,1)S(1)} fusion(f32[3,64]{0,1:T(8,128)S(1)} %broadcast_multiply_fusion, f32[3,64]{0,1:T(8,128)S(1)} %broadcast_multiply_fusion.2, f32[3,64]{0,1:T(8,128)S(1)} %broadcast_multiply_fusion.1, f32[1280]{0:T(1024)S(1)} %copy-done.7, f32[3,64]{0,1:T(8,128)S(1)} %add_rsqrt_fusion, ...), kind=kLoop, calls=%fused_computation.16 | loop fusion | flops 2949120 | bytes 1974272 | tf_op jit(solution)/shard_map/broadcast_in_dim | solution.py:257
  186.2 0.8 copy.41
  187.7 1.3 fusion
  189.8 0.7 reshape.285
  (49 shorter events, 4.4 us)
Async XLA Ops:
  2.2 33.4 %copy-start.3 = (bf16[1,3,64,1280]{3,2,1,0:T(8,128)(2,1)S(1)}, bf16[1,3,64,1280]{3,2,1,0:T(8,128)(2,1)}, u32[]{:S(2)}) copy-start(bf16[1,3,64,1280]{3,2,1,0:T(8,128)(2,1)} %param.10) | copy-start | bytes 1474564
  33.1 37.8 %copy-start.2 = (bf16[8,40,1280]{2,1,0:T(8,128)(2,1)}, bf16[8,40,1280]{2,1,0:T(8,128)(2,1)S(1)}, u32[]{:S(2)}) copy-start(bf16[8,40,1280]{2,1,0:T(8,128)(2,1)S(1)} %all_to_all.25.rest_0_) | copy-start | bytes 2457604
  33.1 24.7 %collective-permute-start.1 = (bf16[8,40,1280]{2,1,0:T(8,128)(2,1)S(1)}, bf16[8,40,1280]{2,1,0:T(8,128)(2,1)}, u32[]{:S(2)}, u32[]{:S(2)}) collective-permute-start(bf16[8,40,1280]{2,1,0:T(8,128)(2,1)S(1)} %all_to_all.25.rest_0_), channel_id=1, source_target_pairs={{0,384},{128,0},{256,128},{384,256},{1,385},{129,1},{257,129},{385... | collective-permute-start | bytes 2457608 | tf_op jit(solution)/shard_map/ppermute | solution.py:169
  36.0 8.4 %copy-start.1 = (bf16[1,3,64,1280]{3,2,1,0:T(8,128)(2,1)S(1)}, bf16[1,3,64,1280]{3,2,1,0:T(8,128)(2,1)}, u32[]{:S(2)}) copy-start(bf16[1,3,64,1280]{3,2,1,0:T(8,128)(2,1)} %param.8) | copy-start | bytes 1474564
  37.4 23.7 %copy-start.7 = (f32[1280]{0:T(1024)S(1)}, f32[1280]{0:T(1024)}, u32[]{:S(2)}) copy-start(f32[1280]{0:T(1024)} %param.11) | copy-start | bytes 15364
  37.4 25.7 %all-to-all-start.1 = ((bf16[64,2,1920]{2,1,0:T(2,128)(2,1)}), bf16[64,2,1920]{2,1,0:T(2,128)(2,1)S(1)}, u32[]{:S(2)}, u32[]{:S(2)}) async-start(bf16[64,2,1920]{2,1,0:T(2,128)(2,1)} %reshape.279), calls=%async_computation.1 | async-start | bytes 983040 | tf_op jit(solution)/shard_map/all_to_all | solution.py:165
  45.5 29.8 %collective-permute-start = (bf16[8,40,1280]{2,1,0:T(8,128)(2,1)S(1)}, bf16[8,40,1280]{2,1,0:T(8,128)(2,1)}, u32[]{:S(2)}, u32[]{:S(2)}) collective-permute-start(bf16[8,40,1280]{2,1,0:T(8,128)(2,1)S(1)} %all_to_all.25.rest_0_), channel_id=1, source_target_pairs={{0,128},{128,256},{256,384},{384,0},{1,129},{129,257},{257,385},{3... | collective-permute-start | bytes 2457608 | tf_op jit(solution)/shard_map/ppermute | solution.py:169
  57.8 19.6 %collective-permute-start.2 = (bf16[8,40,1280]{2,1,0:T(8,128)(2,1)}, bf16[8,40,1280]{2,1,0:T(8,128)(2,1)}, u32[]{:S(2)}, u32[]{:S(2)}) collective-permute-start(bf16[8,40,1280]{2,1,0:T(8,128)(2,1)} %collective-permute-done.1.rest_2_), channel_id=1, source_target_pairs={{0,384},{128,0},{256,128},{384,256},{1,385},{129,1},{257,129},{385... | collective-permute-start | bytes 2457608 | tf_op jit(solution)/shard_map/ppermute | solution.py:169
  63.0 24.2 %all-to-all-start = ((bf16[64,2,1920]{2,1,0:T(2,128)(2,1)}), bf16[64,2,1920]{2,1,0:T(2,128)(2,1)S(1)}, u32[]{:S(2)}, u32[]{:S(2)}) async-start(bf16[64,2,1920]{2,1,0:T(2,128)(2,1)} %reshape.277), calls=%async_computation | async-start | bytes 983040 | tf_op jit(solution)/shard_map/all_to_all | solution.py:165
  71.0 17.4 %collective-permute-start.3 = (bf16[8,40,1280]{2,1,0:T(8,128)(2,1)S(1)}, bf16[8,40,1280]{2,1,0:T(8,128)(2,1)S(1)}, u32[]{:S(2)}, u32[]{:S(2)}) collective-permute-start(bf16[8,40,1280]{2,1,0:T(8,128)(2,1)S(1)} %all_to_all.25.rest_0_), channel_id=1, source_target_pairs={{0,8},{8,0},{1,9},{9,1},{2,10},{10,2},{3,11},{11,3},{4,12},{12,4},... | collective-permute-start | bytes 2457608 | tf_op jit(solution)/shard_map/ppermute | solution.py:169
  73.0 15.3 %collective-permute-start.5 = (bf16[8,40,1280]{2,1,0:T(8,128)(2,1)}, bf16[8,40,1280]{2,1,0:T(8,128)(2,1)}, u32[]{:S(2)}, u32[]{:S(2)}) collective-permute-start(bf16[8,40,1280]{2,1,0:T(8,128)(2,1)} %collective-permute-done.1.rest_2_), channel_id=1, source_target_pairs={{0,8},{8,0},{1,9},{9,1},{2,10},{10,2},{3,11},{11,3},{4,12},{12,4},... | collective-permute-start | bytes 2457608 | tf_op jit(solution)/shard_map/ppermute | solution.py:169
  75.3 13.0 %collective-permute-start.4 = (bf16[8,40,1280]{2,1,0:T(8,128)(2,1)}, bf16[8,40,1280]{2,1,0:T(8,128)(2,1)}, u32[]{:S(2)}, u32[]{:S(2)}) collective-permute-start(bf16[8,40,1280]{2,1,0:T(8,128)(2,1)} %collective-permute-done.rest_1_), channel_id=1, source_target_pairs={{0,8},{8,0},{1,9},{9,1},{2,10},{10,2},{3,11},{11,3},{4,12},{12,4},... | collective-permute-start | bytes 2457608 | tf_op jit(solution)/shard_map/ppermute | solution.py:169
  77.4 11.0 %collective-permute-start.6 = (bf16[8,40,1280]{2,1,0:T(8,128)(2,1)}, bf16[8,40,1280]{2,1,0:T(8,128)(2,1)}, u32[]{:S(2)}, u32[]{:S(2)}) collective-permute-start(bf16[8,40,1280]{2,1,0:T(8,128)(2,1)} %collective-permute-done.2.rest_3_), channel_id=1, source_target_pairs={{0,8},{8,0},{1,9},{9,1},{2,10},{10,2},{3,11},{11,3},{4,12},{12,4},... | collective-permute-start | bytes 2457608 | tf_op jit(solution)/shard_map/ppermute | solution.py:169
  83.5 38.4 %collective-permute-start.8 = (bf16[192,1280]{1,0:T(8,128)(2,1)}, bf16[192,1280]{1,0:T(8,128)(2,1)S(1)}, u32[]{:S(2)}, u32[]{:S(2)}) collective-permute-start(bf16[192,1280]{1,0:T(8,128)(2,1)} %reshape.280.grad_ref), channel_id=1, source_target_pairs={{0,8},{8,0},{1,9},{9,1},{2,10},{10,2},{3,11},{11,3},{4,12},{12,4},... | collective-permute-start | bytes 1474568 | tf_op jit(solution)/shard_map/ppermute | solution.py:169
  88.3 0.9 copy-start.6
  102.6 19.4 %collective-permute-start.7 = (bf16[192,320]{1,0:T(8,128)(2,1)}, bf16[192,320]{1,0:T(8,128)(2,1)S(1)}, u32[]{:S(2)}, u32[]{:S(2)}) collective-permute-start(bf16[192,320]{1,0:T(8,128)(2,1)} %get-tuple-element.21), channel_id=1, source_target_pairs={{0,8},{8,0},{1,9},{9,1},{2,10},{10,2},{3,11},{11,3},{4,12},{12,4},... | collective-permute-start | bytes 368648 | tf_op jit(solution)/shard_map/ppermute | solution.py:169
  104.9 17.0 %copy-start = (bf16[192,320]{1,0:T(8,128)(2,1)S(1)}, bf16[192,320]{1,0:T(8,128)(2,1)}, u32[]{:S(2)}) copy-start(bf16[192,320]{1,0:T(8,128)(2,1)} %get-tuple-element.20.own_ref) | copy-start | bytes 368644
  108.3 60.5 %all-to-all-start.3 = ((bf16[64,2,2880]{2,1,0:T(2,128)(2,1)}), bf16[64,2,2880]{2,1,0:T(2,128)(2,1)}, u32[]{:S(2)}, u32[]{:S(2)}) async-start(bf16[64,2,2880]{2,1,0:T(2,128)(2,1)} %reshape.281), calls=%async_computation.3 | async-start | bytes 1507328 | tf_op jit(solution)/shard_map/all_to_all | solution.py:165
  123.7 14.7 %collective-permute-start.10 = (bf16[80,1280]{1,0:T(8,128)(2,1)S(1)}, bf16[80,1280]{1,0:T(8,128)(2,1)S(1)}, u32[]{:S(2)}, u32[]{:S(2)}) collective-permute-start(bf16[80,1280]{1,0:T(8,128)(2,1)S(1)} %get-tuple-element.24), channel_id=1, source_target_pairs={{0,256},{128,384},{256,0},{384,128},{1,257},{129,385},{257,1},{385... | collective-permute-start | bytes 614408 | tf_op jit(solution)/shard_map/ppermute | solution.py:169
  127.9 16.4 %collective-permute-start.11 = (bf16[80,1280]{1,0:T(8,128)(2,1)S(1)}, bf16[80,1280]{1,0:T(8,128)(2,1)S(1)}, u32[]{:S(2)}, u32[]{:S(2)}) collective-permute-start(bf16[80,1280]{1,0:T(8,128)(2,1)S(1)} %get-tuple-element.25), channel_id=1, source_target_pairs={{0,384},{128,0},{256,128},{384,256},{1,385},{129,1},{257,129},{385... | collective-permute-start | bytes 614408 | tf_op jit(solution)/shard_map/ppermute | solution.py:169
  131.2 13.1 %collective-permute-start.9 = (bf16[80,1280]{1,0:T(8,128)(2,1)S(1)}, bf16[80,1280]{1,0:T(8,128)(2,1)S(1)}, u32[]{:S(2)}, u32[]{:S(2)}) collective-permute-start(bf16[80,1280]{1,0:T(8,128)(2,1)S(1)} %get-tuple-element.23), channel_id=1, source_target_pairs={{0,128},{128,256},{256,384},{384,0},{1,129},{129,257},{257,385},{3... | collective-permute-start | bytes 614408 | tf_op jit(solution)/shard_map/ppermute | solution.py:169
  144.5 6.7 %collective-permute-start.12 = (bf16[40,1280]{1,0:T(8,128)(2,1)S(1)}, bf16[40,1280]{1,0:T(8,128)(2,1)S(1)}, u32[]{:S(2)}, u32[]{:S(2)}) collective-permute-start(bf16[40,1280]{1,0:T(8,128)(2,1)S(1)} %get-tuple-element.27), channel_id=1, source_target_pairs={{0,16},{16,0},{32,48},{48,32},{64,80},{80,64},{96,112},{112,96},{1... | collective-permute-start | bytes 307208 | tf_op jit(solution)/shard_map/ppermute | solution.py:243
  151.2 7.7 %collective-permute-start.13 = (bf16[20,1280]{1,0:T(8,128)(2,1)S(1)}, bf16[20,1280]{1,0:T(8,128)(2,1)S(1)}, u32[]{:S(2)}, u32[]{:S(2)}) collective-permute-start(bf16[20,1280]{1,0:T(8,128)(2,1)S(1)} %get-tuple-element.29), channel_id=1, source_target_pairs={{0,32},{16,48},{32,0},{48,16},{64,96},{80,112},{96,64},{112,80},{1... | collective-permute-start | bytes 153608 | tf_op jit(solution)/shard_map/ppermute | solution.py:243
  158.9 9.8 %collective-permute-start.14 = (bf16[10,1280]{1,0:T(8,128)(2,1)S(1)}, bf16[10,1280]{1,0:T(8,128)(2,1)S(1)}, u32[]{:S(2)}, u32[]{:S(2)}) collective-permute-start(bf16[10,1280]{1,0:T(8,128)(2,1)S(1)} %get-tuple-element.31), channel_id=1, source_target_pairs={{0,64},{16,80},{32,96},{48,112},{64,0},{80,16},{96,32},{112,48},{1... | collective-permute-start | bytes 76808 | tf_op jit(solution)/shard_map/ppermute | solution.py:243
  169.6 20.1 %all-to-all-start.4 = ((bf16[8,2,6400]{2,1,0:T(2,128)(2,1)}), bf16[8,2,6400]{2,1,0:T(2,128)(2,1)S(1)}, u32[]{:S(2)}, u32[]{:S(2)}) async-start(bf16[8,2,6400]{2,1,0:T(2,128)(2,1)} %broadcast_in_dim.17), calls=%async_computation.4 | async-start | bytes 409600 | tf_op jit(solution)/shard_map/all_to_all | solution.py:165
  182.9 1.1 copy-start.4
  186.1 1.6 copy-start.5

commit v3 on v0

--- a/solution.py
+++ b/solution.py
@@ -32,26 +32,23 @@
     low = jnp.bfloat16
     _, lines, depth, _ = whole_ref.shape
     depth //= 2
-    copies = []
     for i, piece in enumerate(pieces):
         step = (0, 3, 1, 2)[i % 4]
         at = lax.rem(place_ref[0] + step, 4) * 2 + lax.rem(place_ref[1] + i // 4, 2)
-        copies.append(pltpu.make_async_copy(piece, whole_ref.at[at], arrived.at[i]))
-    for copy in copies:
-        copy.start()
-    for copy in copies:
-        copy.wait()
+        pltpu.make_async_copy(piece, whole_ref.at[at], arrived.at[at]).start()
+    half = depth // 2
     att, _ = out_ref.shape
     size = att // HEADS
-    half = depth // 2
     scale = 1.0 / math.sqrt(size)
-    for d in range(SIZES[0] * SIZES[1] * SIZES[2]):
-        x, y, core = d // (lines * 2), d // 2 % lines, d % 2
-        piece = whole_ref.at[x * 2 + core, y]
-        qkv_ref[d * depth:(d + 1) * depth, :2 * att] = piece[:depth, :]
-        qkv_ref[d * depth:(d + 1) * depth, 2 * att:] = piece[depth:, :att]
-        out_ref[d * half:(d + 1) * half, :att] = piece[depth:depth + half, att:]
-        out_ref[d * half:(d + 1) * half, att:] = piece[depth + half:, att:]
+    for slot in range(SIZES[0] * SIZES[2]):
+        pltpu.make_async_copy(pieces[0], whole_ref.at[slot], arrived.at[slot]).wait()
+        for y in range(lines):
+            d = (slot // 2 * lines + y) * 2 + slot % 2
+            piece = whole_ref.at[slot, y]
+            qkv_ref[d * depth:(d + 1) * depth, :2 * att] = piece[:depth, :]
+            qkv_ref[d * depth:(d + 1) * depth, 2 * att:] = piece[depth:, :att]
+            out_ref[d * half:(d + 1) * half, :att] = piece[depth:depth + half, att:]
+            out_ref[d * half:(d + 1) * half, att:] = piece[depth + half:, att:]
     qkv = dot(normed_ref[...], qkv_ref[...], NN).astype(low)
     grad_mixed = dot(grad_ref[...], out_ref[...], NT).astype(low)
     same = row_ref[...] == col_ref[...]

time: 185 us -> 185 us (level)
  no operation moved by 1% of the time
where the time goes in v3:
time: 185 us; the launch traced here: 184 us
  starting transfers between devices  77.5 us (42%)
  waiting for transfers between devices  31.9 us (17%)
  blocking collectives  30.8 us (17%)
  local copies, waits for them, and re-layouts  16.6 us (9%)
  Pallas kernels  15.3 us (8%)
  other arithmetic  9.23 us (5%)
    all_to_all x5, starting transfers between devices, exchange(): return lax.all_to_all(values, axis, split_axis=0, concat_axis=0, tiled=True)  45.5 us
    ppermute x12, starting transfers between devices, shift(): lax.ppermute(values, axis, [(i, (i + step) % size) for i in range(size)])  32 us
    all_to_all x1, blocking collectives, exchange(): return lax.all_to_all(values, axis, split_axis=0, concat_axis=0, tiled=True)  30.8 us
    ppermute x12, waiting for transfers between devices, shift(): lax.ppermute(values, axis, [(i, (i + step) % size) for i in range(size)])  18.9 us
    pallas_call x1, Pallas kernels, cell_part(): pl.pallas_call(cell_kernel, out_shape=(jax.ShapeDtypeStruct((rows, att +...  13.5 us
    all_to_all x5, waiting for transfers between devices, exchange(): return lax.all_to_all(values, axis, split_axis=0, concat_axis=0, tiled=True)  13 us
  transfers between devices with their start and end apart: 17, of which 6 were waited for; matrix products, arithmetic and copies ran while one was open for 13% of the time, Pallas kernels for 8%

profile of v3, /device:TPU:2, one launch (start us, length us, event | category | flops | bytes accessed | tf_op | source)
XLA Modules:
  0.0 183.7 jit_solution(6527857761126207409)
XLA Ops:
  0.6 0.8 fusion.24
  1.4 0.8 maximum_maximum_fusion
  2.3 30.8 %all_to_all.30.rest_0_ = bf16[8,40,1280]{2,1,0:T(8,128)(2,1)S(1)} all-to-all(bf16[8,40,1280]{2,1,0:T(8,128)(2,1)S(1)} %broadcast_in_dim.6), channel_id=1, replica_groups=mesh['x'=4,'y'=8,'core'=2,'dp'=8] {'y'}, dimensions={0} | all-to-all | bytes 1638400 | tf_op jit(solution)/shard_map/all_to_all | solution.py:134
  33.1 2.4 %collective-permute-start.1 = (bf16[8,40,1280]{2,1,0:T(8,128)(2,1)S(1)}, bf16[8,40,1280]{2,1,0:T(8,128)(2,1)}, u32[]{:S(2)}, u32[]{:S(2)}) collective-permute-start(bf16[8,40,1280]{2,1,0:T(8,128)(2,1)S(1)} %all_to_all.30.rest_0_), channel_id=1, source_target_pairs={{0,384},{128,0},{256,128},{384,256},{1,385},{129,1},{257,129},{385... | collective-permute-start | bytes 2457608 | tf_op jit(solution)/shard_map/ppermute | solution.py:138
  36.0 1.3 reshape.228
  37.4 7.1 %all-to-all-start.1 = ((bf16[64,2,1920]{2,1,0:T(2,128)(2,1)}), bf16[64,2,1920]{2,1,0:T(2,128)(2,1)S(1)}, u32[]{:S(2)}, u32[]{:S(2)}) async-start(bf16[64,2,1920]{2,1,0:T(2,128)(2,1)} %reshape.228), calls=%async_computation.1 | async-start | bytes 983040 | tf_op jit(solution)/shard_map/all_to_all | solution.py:134
  44.9 0.6 multiply_reduce_fusion.1
  45.5 3.5 %collective-permute-start = (bf16[8,40,1280]{2,1,0:T(8,128)(2,1)S(1)}, bf16[8,40,1280]{2,1,0:T(8,128)(2,1)}, u32[]{:S(2)}, u32[]{:S(2)}) collective-permute-start(bf16[8,40,1280]{2,1,0:T(8,128)(2,1)S(1)} %all_to_all.30.rest_0_), channel_id=1, source_target_pairs={{0,128},{128,256},{256,384},{384,0},{1,129},{129,257},{257,385},{3... | collective-permute-start | bytes 2457608 | tf_op jit(solution)/shard_map/ppermute | solution.py:138
  49.0 8.8 %collective-permute-done.1.rest_2_ = bf16[8,40,1280]{2,1,0:T(8,128)(2,1)} collective-permute-done((bf16[8,40,1280]{2,1,0:T(8,128)(2,1)S(1)}, bf16[8,40,1280]{2,1,0:T(8,128)(2,1)}, u32[]{:S(2)}, u32[]{:S(2)}) %collective-permute-start.1) | collective-permute-done | bytes 819232 | tf_op jit(solution)/shard_map/ppermute | solution.py:138
  57.8 3.2 %collective-permute-start.2 = (bf16[8,40,1280]{2,1,0:T(8,128)(2,1)}, bf16[8,40,1280]{2,1,0:T(8,128)(2,1)}, u32[]{:S(2)}, u32[]{:S(2)}) collective-permute-start(bf16[8,40,1280]{2,1,0:T(8,128)(2,1)} %collective-permute-done.1.rest_2_), channel_id=1, source_target_pairs={{0,384},{128,0},{256,128},{384,256},{1,385},{129,1},{257,129},{385... | collective-permute-start | bytes 2457608 | tf_op jit(solution)/shard_map/ppermute | solution.py:138
  61.1 0.6 fusion.5
  61.7 1.3 reshape.226
  63.0 7.9 %all-to-all-start = ((bf16[64,2,1920]{2,1,0:T(2,128)(2,1)}), bf16[64,2,1920]{2,1,0:T(2,128)(2,1)S(1)}, u32[]{:S(2)}, u32[]{:S(2)}) async-start(bf16[64,2,1920]{2,1,0:T(2,128)(2,1)} %reshape.226), calls=%async_computation | async-start | bytes 983040 | tf_op jit(solution)/shard_map/all_to_all | solution.py:134
  71.0 2.0 %collective-permute-start.3 = (bf16[8,40,1280]{2,1,0:T(8,128)(2,1)S(1)}, bf16[8,40,1280]{2,1,0:T(8,128)(2,1)}, u32[]{:S(2)}, u32[]{:S(2)}) collective-permute-start(bf16[8,40,1280]{2,1,0:T(8,128)(2,1)S(1)} %all_to_all.30.rest_0_), channel_id=1, source_target_pairs={{0,8},{8,0},{1,9},{9,1},{2,10},{10,2},{3,11},{11,3},{4,12},{12,4},... | collective-permute-start | bytes 2457608 | tf_op jit(solution)/shard_map/ppermute | solution.py:138
  73.0 2.3 %collective-permute-start.5 = (bf16[8,40,1280]{2,1,0:T(8,128)(2,1)}, bf16[8,40,1280]{2,1,0:T(8,128)(2,1)}, u32[]{:S(2)}, u32[]{:S(2)}) collective-permute-start(bf16[8,40,1280]{2,1,0:T(8,128)(2,1)} %collective-permute-done.1.rest_2_), channel_id=1, source_target_pairs={{0,8},{8,0},{1,9},{9,1},{2,10},{10,2},{3,11},{11,3},{4,12},{12,4},... | collective-permute-start | bytes 2457608 | tf_op jit(solution)/shard_map/ppermute | solution.py:138
  75.3 2.0 %collective-permute-start.4 = (bf16[8,40,1280]{2,1,0:T(8,128)(2,1)}, bf16[8,40,1280]{2,1,0:T(8,128)(2,1)}, u32[]{:S(2)}, u32[]{:S(2)}) collective-permute-start(bf16[8,40,1280]{2,1,0:T(8,128)(2,1)} %collective-permute-done.rest_1_), channel_id=1, source_target_pairs={{0,8},{8,0},{1,9},{9,1},{2,10},{10,2},{3,11},{11,3},{4,12},{12,4},... | collective-permute-start | bytes 2457608 | tf_op jit(solution)/shard_map/ppermute | solution.py:138
  77.4 2.3 %collective-permute-start.6 = (bf16[8,40,1280]{2,1,0:T(8,128)(2,1)}, bf16[8,40,1280]{2,1,0:T(8,128)(2,1)}, u32[]{:S(2)}, u32[]{:S(2)}) collective-permute-start(bf16[8,40,1280]{2,1,0:T(8,128)(2,1)} %collective-permute-done.2.rest_3_), channel_id=1, source_target_pairs={{0,8},{8,0},{1,9},{9,1},{2,10},{10,2},{3,11},{11,3},{4,12},{12,4},... | collective-permute-start | bytes 2457608 | tf_op jit(solution)/shard_map/ppermute | solution.py:138
  79.7 1.3 dynamic-slice_bitcast_fusion
  81.0 0.8 copy.38.row_ref
  82.1 1.2 add_convert_fusion.pick_ref
  83.3 1.1 reshape.229.grad_ref
  84.4 2.2 %collective-permute-start.8 = (bf16[192,1280]{1,0:T(8,128)(2,1)}, bf16[192,1280]{1,0:T(8,128)(2,1)S(1)}, u32[]{:S(2)}, u32[]{:S(2)}) collective-permute-start(bf16[192,1280]{1,0:T(8,128)(2,1)} %reshape.229.grad_ref), channel_id=1, source_target_pairs={{0,8},{8,0},{1,9},{9,1},{2,10},{10,2},{3,11},{11,3},{4,12},{12,4},... | collective-permute-start | bytes 1474568 | tf_op jit(solution)/shard_map/ppermute | solution.py:138
  86.6 0.6 pad_add_fusion.place_ref
  87.2 1.1 reshape.227.normed_ref
  88.3 13.5 %shard_map.103 = (bf16[192,1920]{1,0:T(8,128)(2,1)}, bf16[192,320]{1,0:T(8,128)(2,1)}, bf16[192,320]{1,0:T(8,128)(2,1)}, bf16[640,1280]{1,0:T(8,128)(2,1)}) custom-call(s32[2]{0:T(128)} %pad_add_fusion.place_ref, bf16[192,1280]{1,0:T(8,128)(2,1)} %reshape.227.normed_ref, bf16[192,1280]{1,0:T(8,128)(2,1)} %reshape.229.grad_ref, s32[192,1]{1,0:T(8,128)} %copy.38.row_ref, ...), custom_call_target="tpu_custom_call" | custom-call | tf_op jit(solution)/shard_map/pallas_call | solution.py:84
  101.9 3.4 %reshape.230 = bf16[64,2,2880]{2,1,0:T(2,128)(2,1)} reshape(bf16[192,1920]{1,0:T(8,128)(2,1)} %get-tuple-element.12) | data formatting | bytes 1474560 | tf_op jit(solution)/shard_map/reshape | solution.py:198
  105.2 14.0 %all-to-all-start.3 = ((bf16[64,2,2880]{2,1,0:T(2,128)(2,1)}), bf16[64,2,2880]{2,1,0:T(2,128)(2,1)S(1)}, u32[]{:S(2)}, u32[]{:S(2)}) async-start(bf16[64,2,2880]{2,1,0:T(2,128)(2,1)} %reshape.230), calls=%async_computation.3 | async-start | bytes 1507328 | tf_op jit(solution)/shard_map/all_to_all | solution.py:134
  119.3 2.0 %collective-permute-start.7 = (bf16[192,320]{1,0:T(8,128)(2,1)S(1)}, bf16[192,320]{1,0:T(8,128)(2,1)S(1)}, u32[]{:S(2)}, u32[]{:S(2)}) collective-permute-start(bf16[192,320]{1,0:T(8,128)(2,1)S(1)} %copy-done.6), channel_id=1, source_target_pairs={{0,8},{8,0},{1,9},{9,1},{2,10},{10,2},{3,11},{11,3},{4,12},{12,4},... | collective-permute-start | bytes 368648 | tf_op jit(solution)/shard_map/ppermute | solution.py:138
  121.3 1.2 collective-permute-done.7.got_ref
  122.5 1.8 shard_map.104
  124.3 4.2 %collective-permute-start.10 = (bf16[80,1280]{1,0:T(8,128)(2,1)S(1)}, bf16[80,1280]{1,0:T(8,128)(2,1)S(1)}, u32[]{:S(2)}, u32[]{:S(2)}) collective-permute-start(bf16[80,1280]{1,0:T(8,128)(2,1)S(1)} %get-tuple-element.18), channel_id=1, source_target_pairs={{0,256},{128,384},{256,0},{384,128},{1,257},{129,385},{257,1},{385... | collective-permute-start | bytes 614408 | tf_op jit(solution)/shard_map/ppermute | solution.py:138
  128.5 3.3 %collective-permute-start.11 = (bf16[80,1280]{1,0:T(8,128)(2,1)S(1)}, bf16[80,1280]{1,0:T(8,128)(2,1)S(1)}, u32[]{:S(2)}, u32[]{:S(2)}) collective-permute-start(bf16[80,1280]{1,0:T(8,128)(2,1)S(1)} %get-tuple-element.19), channel_id=1, source_target_pairs={{0,384},{128,0},{256,128},{384,256},{1,385},{129,1},{257,129},{385... | collective-permute-start | bytes 614408 | tf_op jit(solution)/shard_map/ppermute | solution.py:138
  131.8 2.6 %collective-permute-start.9 = (bf16[80,1280]{1,0:T(8,128)(2,1)S(1)}, bf16[80,1280]{1,0:T(8,128)(2,1)S(1)}, u32[]{:S(2)}, u32[]{:S(2)}) collective-permute-start(bf16[80,1280]{1,0:T(8,128)(2,1)S(1)} %get-tuple-element.17), channel_id=1, source_target_pairs={{0,128},{128,256},{256,384},{384,0},{1,129},{129,257},{257,385},{3... | collective-permute-start | bytes 614408 | tf_op jit(solution)/shard_map/ppermute | solution.py:138
  135.0 4.7 %collective-permute-done.10 = bf16[80,1280]{1,0:T(8,128)(2,1)S(1)} collective-permute-done((bf16[80,1280]{1,0:T(8,128)(2,1)S(1)}, bf16[80,1280]{1,0:T(8,128)(2,1)S(1)}, u32[]{:S(2)}, u32[]{:S(2)}) %collective-permute-start.10) | collective-permute-done | bytes 204832 | tf_op jit(solution)/shard_map/ppermute | solution.py:138
  139.6 4.2 %collective-permute-done.11 = bf16[80,1280]{1,0:T(8,128)(2,1)S(1)} collective-permute-done((bf16[80,1280]{1,0:T(8,128)(2,1)S(1)}, bf16[80,1280]{1,0:T(8,128)(2,1)S(1)}, u32[]{:S(2)}, u32[]{:S(2)}) %collective-permute-start.11) | collective-permute-done | bytes 204832 | tf_op jit(solution)/shard_map/ppermute | solution.py:138
  143.9 0.8 reshape.233
  144.7 6.3 %all-to-all-start.4 = ((bf16[8,2,6400]{2,1,0:T(2,128)(2,1)}), bf16[8,2,6400]{2,1,0:T(2,128)(2,1)S(1)}, u32[]{:S(2)}, u32[]{:S(2)}) async-start(bf16[8,2,6400]{2,1,0:T(2,128)(2,1)} %reshape.233), calls=%async_computation.4 | async-start | bytes 409600 | tf_op jit(solution)/shard_map/all_to_all | solution.py:134
  151.0 1.1 reshape.231
  152.1 1.1 fusion.1
  153.2 8.7 %all-to-all-done.4 = bf16[8,2,6400]{2,1,0:T(2,128)(2,1)S(1)} async-done(((bf16[8,2,6400]{2,1,0:T(2,128)(2,1)}), bf16[8,2,6400]{2,1,0:T(2,128)(2,1)S(1)}, u32[]{:S(2)}, u32[]{:S(2)}) %all-to-all-start.4) | async-done | bytes 204832 | tf_op jit(solution)/shard_map/all_to_all | solution.py:134
  162.1 0.8 broadcast_in_dim.8
  162.8 10.2 %all-to-all-start.5 = ((bf16[8,2,6400]{2,1,0:T(2,128)(2,1)}), bf16[8,2,6400]{2,1,0:T(2,128)(2,1)S(1)}, u32[]{:S(2)}, u32[]{:S(2)}) async-start(bf16[8,2,6400]{2,1,0:T(2,128)(2,1)} %broadcast_in_dim.8), calls=%async_computation.5 | async-start | bytes 409600 | tf_op jit(solution)/shard_map/all_to_all | solution.py:134
  173.0 2.6 %fusion.6 = bf16[1,3,64,1280]{3,1,2,0:T(4,128)(2,1)S(1)} fusion(f32[3,64]{0,1:T(8,128)S(1)} %broadcast_multiply_fusion, f32[3,64]{0,1:T(8,128)S(1)} %broadcast_multiply_fusion.2, f32[3,64]{0,1:T(8,128)S(1)} %broadcast_multiply_fusion.1, f32[1280]{0:T(1024)S(1)} %copy-done.5, f32[3,64]{0,1:T(8,128)S(1)} %add_rsqrt_fusion, bf16[1,3,64,1280]{3,2,1,0:T(8,128)(2,1)} %param.10, ...), kind=kLoop, calls=%fused_computation.16 | loop fusion | flops 2949120 | bytes 1974272 | tf_op jit(solution)/shard_map/broadcast_in_dim | solution.py:222
  175.8 0.8 copy.41
  176.6 0.6 copy-done.4
  177.3 1.3 fusion
  178.6 4.3 %all-to-all-done.5 = bf16[8,2,6400]{2,1,0:T(2,128)(2,1)S(1)} async-done(((bf16[8,2,6400]{2,1,0:T(2,128)(2,1)}), bf16[8,2,6400]{2,1,0:T(2,128)(2,1)S(1)}, u32[]{:S(2)}, u32[]{:S(2)}) %all-to-all-start.5) | async-done | bytes 204832 | tf_op jit(solution)/shard_map/all_to_all | solution.py:134
  183.0 0.7 reshape.234
  (41 shorter events, 2.6 us)
Async XLA Ops:
  2.2 33.4 %copy-start.3 = (bf16[1,3,64,1280]{3,2,1,0:T(8,128)(2,1)S(1)}, bf16[1,3,64,1280]{3,2,1,0:T(8,128)(2,1)}, u32[]{:S(2)}) copy-start(bf16[1,3,64,1280]{3,2,1,0:T(8,128)(2,1)} %param.10) | copy-start | bytes 1474564
  33.1 37.8 %copy-start.2 = (bf16[8,40,1280]{2,1,0:T(8,128)(2,1)}, bf16[8,40,1280]{2,1,0:T(8,128)(2,1)S(1)}, u32[]{:S(2)}) copy-start(bf16[8,40,1280]{2,1,0:T(8,128)(2,1)S(1)} %all_to_all.30.rest_0_) | copy-start | bytes 2457604
  33.1 24.7 %collective-permute-start.1 = (bf16[8,40,1280]{2,1,0:T(8,128)(2,1)S(1)}, bf16[8,40,1280]{2,1,0:T(8,128)(2,1)}, u32[]{:S(2)}, u32[]{:S(2)}) collective-permute-start(bf16[8,40,1280]{2,1,0:T(8,128)(2,1)S(1)} %all_to_all.30.rest_0_), channel_id=1, source_target_pairs={{0,384},{128,0},{256,128},{384,256},{1,385},{129,1},{257,129},{385... | collective-permute-start | bytes 2457608 | tf_op jit(solution)/shard_map/ppermute | solution.py:138
  36.0 8.4 %copy-start.1 = (bf16[1,3,64,1280]{3,2,1,0:T(8,128)(2,1)S(1)}, bf16[1,3,64,1280]{3,2,1,0:T(8,128)(2,1)}, u32[]{:S(2)}) copy-start(bf16[1,3,64,1280]{3,2,1,0:T(8,128)(2,1)} %param.8) | copy-start | bytes 1474564
  37.4 23.7 %copy-start.5 = (f32[1280]{0:T(1024)S(1)}, f32[1280]{0:T(1024)}, u32[]{:S(2)}) copy-start(f32[1280]{0:T(1024)} %param.11) | copy-start | bytes 15364
  37.4 25.7 %all-to-all-start.1 = ((bf16[64,2,1920]{2,1,0:T(2,128)(2,1)}), bf16[64,2,1920]{2,1,0:T(2,128)(2,1)S(1)}, u32[]{:S(2)}, u32[]{:S(2)}) async-start(bf16[64,2,1920]{2,1,0:T(2,128)(2,1)} %reshape.228), calls=%async_computation.1 | async-start | bytes 983040 | tf_op jit(solution)/shard_map/all_to_all | solution.py:134
  45.5 29.8 %collective-permute-start = (bf16[8,40,1280]{2,1,0:T(8,128)(2,1)S(1)}, bf16[8,40,1280]{2,1,0:T(8,128)(2,1)}, u32[]{:S(2)}, u32[]{:S(2)}) collective-permute-start(bf16[8,40,1280]{2,1,0:T(8,128)(2,1)S(1)} %all_to_all.30.rest_0_), channel_id=1, source_target_pairs={{0,128},{128,256},{256,384},{384,0},{1,129},{129,257},{257,385},{3... | collective-permute-start | bytes 2457608 | tf_op jit(solution)/shard_map/ppermute | solution.py:138
  57.8 19.6 %collective-permute-start.2 = (bf16[8,40,1280]{2,1,0:T(8,128)(2,1)}, bf16[8,40,1280]{2,1,0:T(8,128)(2,1)}, u32[]{:S(2)}, u32[]{:S(2)}) collective-permute-start(bf16[8,40,1280]{2,1,0:T(8,128)(2,1)} %collective-permute-done.1.rest_2_), channel_id=1, source_target_pairs={{0,384},{128,0},{256,128},{384,256},{1,385},{129,1},{257,129},{385... | collective-permute-start | bytes 2457608 | tf_op jit(solution)/shard_map/ppermute | solution.py:138
  63.0 24.2 %all-to-all-start = ((bf16[64,2,1920]{2,1,0:T(2,128)(2,1)}), bf16[64,2,1920]{2,1,0:T(2,128)(2,1)S(1)}, u32[]{:S(2)}, u32[]{:S(2)}) async-start(bf16[64,2,1920]{2,1,0:T(2,128)(2,1)} %reshape.226), calls=%async_computation | async-start | bytes 983040 | tf_op jit(solution)/shard_map/all_to_all | solution.py:134
  71.0 17.3 %collective-permute-start.3 = (bf16[8,40,1280]{2,1,0:T(8,128)(2,1)S(1)}, bf16[8,40,1280]{2,1,0:T(8,128)(2,1)}, u32[]{:S(2)}, u32[]{:S(2)}) collective-permute-start(bf16[8,40,1280]{2,1,0:T(8,128)(2,1)S(1)} %all_to_all.30.rest_0_), channel_id=1, source_target_pairs={{0,8},{8,0},{1,9},{9,1},{2,10},{10,2},{3,11},{11,3},{4,12},{12,4},... | collective-permute-start | bytes 2457608 | tf_op jit(solution)/shard_map/ppermute | solution.py:138
  73.0 15.3 %collective-permute-start.5 = (bf16[8,40,1280]{2,1,0:T(8,128)(2,1)}, bf16[8,40,1280]{2,1,0:T(8,128)(2,1)}, u32[]{:S(2)}, u32[]{:S(2)}) collective-permute-start(bf16[8,40,1280]{2,1,0:T(8,128)(2,1)} %collective-permute-done.1.rest_2_), channel_id=1, source_target_pairs={{0,8},{8,0},{1,9},{9,1},{2,10},{10,2},{3,11},{11,3},{4,12},{12,4},... | collective-permute-start | bytes 2457608 | tf_op jit(solution)/shard_map/ppermute | solution.py:138
  75.3 13.0 %collective-permute-start.4 = (bf16[8,40,1280]{2,1,0:T(8,128)(2,1)}, bf16[8,40,1280]{2,1,0:T(8,128)(2,1)}, u32[]{:S(2)}, u32[]{:S(2)}) collective-permute-start(bf16[8,40,1280]{2,1,0:T(8,128)(2,1)} %collective-permute-done.rest_1_), channel_id=1, source_target_pairs={{0,8},{8,0},{1,9},{9,1},{2,10},{10,2},{3,11},{11,3},{4,12},{12,4},... | collective-permute-start | bytes 2457608 | tf_op jit(solution)/shard_map/ppermute | solution.py:138
  77.4 10.9 %collective-permute-start.6 = (bf16[8,40,1280]{2,1,0:T(8,128)(2,1)}, bf16[8,40,1280]{2,1,0:T(8,128)(2,1)}, u32[]{:S(2)}, u32[]{:S(2)}) collective-permute-start(bf16[8,40,1280]{2,1,0:T(8,128)(2,1)} %collective-permute-done.2.rest_3_), channel_id=1, source_target_pairs={{0,8},{8,0},{1,9},{9,1},{2,10},{10,2},{3,11},{11,3},{4,12},{12,4},... | collective-permute-start | bytes 2457608 | tf_op jit(solution)/shard_map/ppermute | solution.py:138
  84.4 36.9 %collective-permute-start.8 = (bf16[192,1280]{1,0:T(8,128)(2,1)}, bf16[192,1280]{1,0:T(8,128)(2,1)S(1)}, u32[]{:S(2)}, u32[]{:S(2)}) collective-permute-start(bf16[192,1280]{1,0:T(8,128)(2,1)} %reshape.229.grad_ref), channel_id=1, source_target_pairs={{0,8},{8,0},{1,9},{9,1},{2,10},{10,2},{3,11},{11,3},{4,12},{12,4},... | collective-permute-start | bytes 1474568 | tf_op jit(solution)/shard_map/ppermute | solution.py:138
  101.8 17.4 %copy-start.6 = (bf16[192,320]{1,0:T(8,128)(2,1)S(1)}, bf16[192,320]{1,0:T(8,128)(2,1)}, u32[]{:S(2)}) copy-start(bf16[192,320]{1,0:T(8,128)(2,1)} %get-tuple-element.15) | copy-start | bytes 368644
  101.8 20.7 %copy-start = (bf16[192,320]{1,0:T(8,128)(2,1)S(1)}, bf16[192,320]{1,0:T(8,128)(2,1)}, u32[]{:S(2)}) copy-start(bf16[192,320]{1,0:T(8,128)(2,1)} %get-tuple-element.14.own_ref) | copy-start | bytes 368644
  105.2 39.5 %all-to-all-start.3 = ((bf16[64,2,2880]{2,1,0:T(2,128)(2,1)}), bf16[64,2,2880]{2,1,0:T(2,128)(2,1)S(1)}, u32[]{:S(2)}, u32[]{:S(2)}) async-start(bf16[64,2,2880]{2,1,0:T(2,128)(2,1)} %reshape.230), calls=%async_computation.3 | async-start | bytes 1507328 | tf_op jit(solution)/shard_map/all_to_all | solution.py:134
  119.3 3.3 %collective-permute-start.7 = (bf16[192,320]{1,0:T(8,128)(2,1)S(1)}, bf16[192,320]{1,0:T(8,128)(2,1)S(1)}, u32[]{:S(2)}, u32[]{:S(2)}) collective-permute-start(bf16[192,320]{1,0:T(8,128)(2,1)S(1)} %copy-done.6), channel_id=1, source_target_pairs={{0,8},{8,0},{1,9},{9,1},{2,10},{10,2},{3,11},{11,3},{4,12},{12,4},... | collective-permute-start | bytes 368648 | tf_op jit(solution)/shard_map/ppermute | solution.py:138
  124.3 15.3 %collective-permute-start.10 = (bf16[80,1280]{1,0:T(8,128)(2,1)S(1)}, bf16[80,1280]{1,0:T(8,128)(2,1)S(1)}, u32[]{:S(2)}, u32[]{:S(2)}) collective-permute-start(bf16[80,1280]{1,0:T(8,128)(2,1)S(1)} %get-tuple-element.18), channel_id=1, source_target_pairs={{0,256},{128,384},{256,0},{384,128},{1,257},{129,385},{257,1},{385... | collective-permute-start | bytes 614408 | tf_op jit(solution)/shard_map/ppermute | solution.py:138
  128.5 15.3 %collective-permute-start.11 = (bf16[80,1280]{1,0:T(8,128)(2,1)S(1)}, bf16[80,1280]{1,0:T(8,128)(2,1)S(1)}, u32[]{:S(2)}, u32[]{:S(2)}) collective-permute-start(bf16[80,1280]{1,0:T(8,128)(2,1)S(1)} %get-tuple-element.19), channel_id=1, source_target_pairs={{0,384},{128,0},{256,128},{384,256},{1,385},{129,1},{257,129},{385... | collective-permute-start | bytes 614408 | tf_op jit(solution)/shard_map/ppermute | solution.py:138
  131.8 12.1 %collective-permute-start.9 = (bf16[80,1280]{1,0:T(8,128)(2,1)S(1)}, bf16[80,1280]{1,0:T(8,128)(2,1)S(1)}, u32[]{:S(2)}, u32[]{:S(2)}) collective-permute-start(bf16[80,1280]{1,0:T(8,128)(2,1)S(1)} %get-tuple-element.17), channel_id=1, source_target_pairs={{0,128},{128,256},{256,384},{384,0},{1,129},{129,257},{257,385},{3... | collective-permute-start | bytes 614408 | tf_op jit(solution)/shard_map/ppermute | solution.py:138
  144.7 17.2 %all-to-all-start.4 = ((bf16[8,2,6400]{2,1,0:T(2,128)(2,1)}), bf16[8,2,6400]{2,1,0:T(2,128)(2,1)S(1)}, u32[]{:S(2)}, u32[]{:S(2)}) async-start(bf16[8,2,6400]{2,1,0:T(2,128)(2,1)} %reshape.233), calls=%async_computation.4 | async-start | bytes 409600 | tf_op jit(solution)/shard_map/all_to_all | solution.py:134
  162.8 20.0 %all-to-all-start.5 = ((bf16[8,2,6400]{2,1,0:T(2,128)(2,1)}), bf16[8,2,6400]{2,1,0:T(2,128)(2,1)S(1)}, u32[]{:S(2)}, u32[]{:S(2)}) async-start(bf16[8,2,6400]{2,1,0:T(2,128)(2,1)} %broadcast_in_dim.8), calls=%async_computation.5 | async-start | bytes 409600 | tf_op jit(solution)/shard_map/all_to_all | solution.py:134
  175.6 1.6 copy-start.4

commit v4 on v0

--- a/solution.py
+++ b/solution.py
@@ -56,22 +56,31 @@
     grad_mixed = dot(grad_ref[...], out_ref[...], NT).astype(low)
     same = row_ref[...] == col_ref[...]
     mixed, grad_q, grad_k, grad_v = [], [], [], []
-    for h in range(HEADS):
-        q = qkv[:, h * size:(h + 1) * size]
-        k = qkv[:, att + h * size:att + (h + 1) * size]
-        v = qkv[:, 2 * att + h * size:2 * att + (h + 1) * size]
-        g = grad_mixed[:, h * size:(h + 1) * size]
-        scores = jnp.where(same, dot(q, k, NT) * scale, -jnp.inf)
-        expons = jnp.exp(scores - jnp.max(scores, axis=-1, keepdims=True))
-        probs = expons / jnp.sum(expons, axis=-1, keepdims=True)
-        probs_low = probs.astype(low)
-        mixed.append(dot(probs_low, v, NN).astype(low))
-        grad_probs = dot(g, v, NT)
-        centre = jnp.sum(probs * grad_probs, axis=-1, keepdims=True)
-        grad_scores = (probs * (grad_probs - centre) * scale).astype(low)
-        grad_q.append(dot(grad_scores, k, NN).astype(low))
-        grad_k.append(dot(grad_scores, q, TN).astype(low))
-        grad_v.append(dot(probs_low, g, TN).astype(low))
+    for first in range(0, HEADS, 4):
+        heads = range(first, first + 4)
+        q = [qkv[:, h * size:(h + 1) * size] for h in heads]
+        k = [qkv[:, att + h * size:att + (h + 1) * size] for h in heads]
+        v = [qkv[:, 2 * att + h * size:2 * att + (h + 1) * size] for h in heads]
+        g = [grad_mixed[:, h * size:(h + 1) * size] for h in heads]
+        scores = [dot(a, b, NT) for a, b in zip(q, k)]
+        grad_probs = [dot(a, b, NT) for a, b in zip(g, v)]
+        scores = [jnp.where(same, a * scale, -jnp.inf) for a in scores]
+        tops = [jnp.max(a, axis=-1, keepdims=True) for a in scores]
+        expons = [jnp.exp(a - b) for a, b in zip(scores, tops)]
+        sums = [jnp.sum(a, axis=-1, keepdims=True) for a in expons]
+        probs = [a * pl.reciprocal(b) for a, b in zip(expons, sums)]
+        probs_low = [a.astype(low) for a in probs]
+        mixed += [dot(a, b, NN).astype(low) for a, b in zip(probs_low, v)]
+        grad_v += [dot(a, b, TN).astype(low) for a, b in zip(probs_low, g)]
+        centres = [
+            jnp.sum(a * b, axis=-1, keepdims=True) for a, b in zip(probs, grad_probs)
+        ]
+        grad_scores = [
+            (a * (b - c) * scale).astype(low)
+            for a, b, c in zip(probs, grad_probs, centres)
+        ]
+        grad_q += [dot(a, b, NN).astype(low) for a, b in zip(grad_scores, k)]
+        grad_k += [dot(a, b, TN).astype(low) for a, b in zip(grad_scores, q)]
     mixed = jnp.concatenate(mixed, axis=1)
     sent_ref[:, :att] = mixed
     own_ref[...] = dot(mixed, pick_ref[0], NN).astype(low)

time: 185 us -> 184 us (level)
  no operation moved by 1% of the time
where the time goes in v4:
time: 184 us; the launch traced here: 183 us
  starting transfers between devices  77.3 us (42%)
  waiting for transfers between devices  31.9 us (17%)
  blocking collectives  30.8 us (17%)
  local copies, waits for them, and re-layouts  16.6 us (9%)
  Pallas kernels  14.6 us (8%)
  other arithmetic  9.23 us (5%)
    all_to_all x5, starting transfers between devices, exchange(): return lax.all_to_all(values, axis, split_axis=0, concat_axis=0, tiled=True)  45.3 us
    ppermute x12, starting transfers between devices, shift(): lax.ppermute(values, axis, [(i, (i + step) % size) for i in range(size)])  32 us
    all_to_all x1, blocking collectives, exchange(): return lax.all_to_all(values, axis, split_axis=0, concat_axis=0, tiled=True)  30.8 us
    ppermute x12, waiting for transfers between devices, shift(): lax.ppermute(values, axis, [(i, (i + step) % size) for i in range(size)])  18.9 us
    all_to_all x5, waiting for transfers between devices, exchange(): return lax.all_to_all(values, axis, split_axis=0, concat_axis=0, tiled=True)  13 us
    pallas_call x1, Pallas kernels, cell_part(): pl.pallas_call(cell_kernel, out_shape=(jax.ShapeDtypeStruct((rows, att +...  12.8 us
  transfers between devices with their start and end apart: 17, of which 6 were waited for; matrix products, arithmetic and copies ran while one was open for 13% of the time, Pallas kernels for 8%

profile of v4, /device:TPU:2, one launch (start us, length us, event | category | flops | bytes accessed | tf_op | source)
XLA Modules:
  0.0 182.7 jit_solution(2678455068543946079)
XLA Ops:
  0.6 0.8 fusion.24
  1.4 0.8 maximum_maximum_fusion
  2.3 30.8 %all_to_all.30.rest_0_ = bf16[8,40,1280]{2,1,0:T(8,128)(2,1)S(1)} all-to-all(bf16[8,40,1280]{2,1,0:T(8,128)(2,1)S(1)} %broadcast_in_dim.6), channel_id=1, replica_groups=mesh['x'=4,'y'=8,'core'=2,'dp'=8] {'y'}, dimensions={0} | all-to-all | bytes 1638400 | tf_op jit(solution)/shard_map/all_to_all | solution.py:146
  33.1 2.4 %collective-permute-start.1 = (bf16[8,40,1280]{2,1,0:T(8,128)(2,1)S(1)}, bf16[8,40,1280]{2,1,0:T(8,128)(2,1)}, u32[]{:S(2)}, u32[]{:S(2)}) collective-permute-start(bf16[8,40,1280]{2,1,0:T(8,128)(2,1)S(1)} %all_to_all.30.rest_0_), channel_id=1, source_target_pairs={{0,384},{128,0},{256,128},{384,256},{1,385},{129,1},{257,129},{385... | collective-permute-start | bytes 2457608 | tf_op jit(solution)/shard_map/ppermute | solution.py:150
  36.0 1.3 reshape.228
  37.4 7.1 %all-to-all-start.1 = ((bf16[64,2,1920]{2,1,0:T(2,128)(2,1)}), bf16[64,2,1920]{2,1,0:T(2,128)(2,1)S(1)}, u32[]{:S(2)}, u32[]{:S(2)}) async-start(bf16[64,2,1920]{2,1,0:T(2,128)(2,1)} %reshape.228), calls=%async_computation.1 | async-start | bytes 983040 | tf_op jit(solution)/shard_map/all_to_all | solution.py:146
  44.9 0.6 multiply_reduce_fusion.1
  45.5 3.5 %collective-permute-start = (bf16[8,40,1280]{2,1,0:T(8,128)(2,1)S(1)}, bf16[8,40,1280]{2,1,0:T(8,128)(2,1)}, u32[]{:S(2)}, u32[]{:S(2)}) collective-permute-start(bf16[8,40,1280]{2,1,0:T(8,128)(2,1)S(1)} %all_to_all.30.rest_0_), channel_id=1, source_target_pairs={{0,128},{128,256},{256,384},{384,0},{1,129},{129,257},{257,385},{3... | collective-permute-start | bytes 2457608 | tf_op jit(solution)/shard_map/ppermute | solution.py:150
  49.0 8.8 %collective-permute-done.1.rest_2_ = bf16[8,40,1280]{2,1,0:T(8,128)(2,1)} collective-permute-done((bf16[8,40,1280]{2,1,0:T(8,128)(2,1)S(1)}, bf16[8,40,1280]{2,1,0:T(8,128)(2,1)}, u32[]{:S(2)}, u32[]{:S(2)}) %collective-permute-start.1) | collective-permute-done | bytes 819232 | tf_op jit(solution)/shard_map/ppermute | solution.py:150
  57.8 3.2 %collective-permute-start.2 = (bf16[8,40,1280]{2,1,0:T(8,128)(2,1)}, bf16[8,40,1280]{2,1,0:T(8,128)(2,1)}, u32[]{:S(2)}, u32[]{:S(2)}) collective-permute-start(bf16[8,40,1280]{2,1,0:T(8,128)(2,1)} %collective-permute-done.1.rest_2_), channel_id=1, source_target_pairs={{0,384},{128,0},{256,128},{384,256},{1,385},{129,1},{257,129},{385... | collective-permute-start | bytes 2457608 | tf_op jit(solution)/shard_map/ppermute | solution.py:150
  61.1 0.6 fusion.5
  61.7 1.3 reshape.226
  63.0 7.9 %all-to-all-start = ((bf16[64,2,1920]{2,1,0:T(2,128)(2,1)}), bf16[64,2,1920]{2,1,0:T(2,128)(2,1)S(1)}, u32[]{:S(2)}, u32[]{:S(2)}) async-start(bf16[64,2,1920]{2,1,0:T(2,128)(2,1)} %reshape.226), calls=%async_computation | async-start | bytes 983040 | tf_op jit(solution)/shard_map/all_to_all | solution.py:146
  71.0 2.0 %collective-permute-start.3 = (bf16[8,40,1280]{2,1,0:T(8,128)(2,1)S(1)}, bf16[8,40,1280]{2,1,0:T(8,128)(2,1)}, u32[]{:S(2)}, u32[]{:S(2)}) collective-permute-start(bf16[8,40,1280]{2,1,0:T(8,128)(2,1)S(1)} %all_to_all.30.rest_0_), channel_id=1, source_target_pairs={{0,8},{8,0},{1,9},{9,1},{2,10},{10,2},{3,11},{11,3},{4,12},{12,4},... | collective-permute-start | bytes 2457608 | tf_op jit(solution)/shard_map/ppermute | solution.py:150
  73.0 2.3 %collective-permute-start.5 = (bf16[8,40,1280]{2,1,0:T(8,128)(2,1)}, bf16[8,40,1280]{2,1,0:T(8,128)(2,1)}, u32[]{:S(2)}, u32[]{:S(2)}) collective-permute-start(bf16[8,40,1280]{2,1,0:T(8,128)(2,1)} %collective-permute-done.1.rest_2_), channel_id=1, source_target_pairs={{0,8},{8,0},{1,9},{9,1},{2,10},{10,2},{3,11},{11,3},{4,12},{12,4},... | collective-permute-start | bytes 2457608 | tf_op jit(solution)/shard_map/ppermute | solution.py:150
  75.3 2.0 %collective-permute-start.4 = (bf16[8,40,1280]{2,1,0:T(8,128)(2,1)}, bf16[8,40,1280]{2,1,0:T(8,128)(2,1)}, u32[]{:S(2)}, u32[]{:S(2)}) collective-permute-start(bf16[8,40,1280]{2,1,0:T(8,128)(2,1)} %collective-permute-done.rest_1_), channel_id=1, source_target_pairs={{0,8},{8,0},{1,9},{9,1},{2,10},{10,2},{3,11},{11,3},{4,12},{12,4},... | collective-permute-start | bytes 2457608 | tf_op jit(solution)/shard_map/ppermute | solution.py:150
  77.4 2.3 %collective-permute-start.6 = (bf16[8,40,1280]{2,1,0:T(8,128)(2,1)}, bf16[8,40,1280]{2,1,0:T(8,128)(2,1)}, u32[]{:S(2)}, u32[]{:S(2)}) collective-permute-start(bf16[8,40,1280]{2,1,0:T(8,128)(2,1)} %collective-permute-done.2.rest_3_), channel_id=1, source_target_pairs={{0,8},{8,0},{1,9},{9,1},{2,10},{10,2},{3,11},{11,3},{4,12},{12,4},... | collective-permute-start | bytes 2457608 | tf_op jit(solution)/shard_map/ppermute | solution.py:150
  79.7 1.3 dynamic-slice_bitcast_fusion
  81.0 0.8 copy.38.row_ref
  82.1 1.2 add_convert_fusion.pick_ref
  83.3 1.1 reshape.229.grad_ref
  84.4 2.2 %collective-permute-start.8 = (bf16[192,1280]{1,0:T(8,128)(2,1)}, bf16[192,1280]{1,0:T(8,128)(2,1)S(1)}, u32[]{:S(2)}, u32[]{:S(2)}) collective-permute-start(bf16[192,1280]{1,0:T(8,128)(2,1)} %reshape.229.grad_ref), channel_id=1, source_target_pairs={{0,8},{8,0},{1,9},{9,1},{2,10},{10,2},{3,11},{11,3},{4,12},{12,4},... | collective-permute-start | bytes 1474568 | tf_op jit(solution)/shard_map/ppermute | solution.py:150
  86.6 0.6 pad_add_fusion.place_ref
  87.2 1.1 reshape.227.normed_ref
  88.3 12.8 %shard_map.103 = (bf16[192,1920]{1,0:T(8,128)(2,1)}, bf16[192,320]{1,0:T(8,128)(2,1)}, bf16[192,320]{1,0:T(8,128)(2,1)}, bf16[640,1280]{1,0:T(8,128)(2,1)}) custom-call(s32[2]{0:T(128)} %pad_add_fusion.place_ref, bf16[192,1280]{1,0:T(8,128)(2,1)} %reshape.227.normed_ref, bf16[192,1280]{1,0:T(8,128)(2,1)} %reshape.229.grad_ref, s32[192,1]{1,0:T(8,128)} %copy.38.row_ref, ...), custom_call_target="tpu_custom_call" | custom-call | tf_op jit(solution)/shard_map/pallas_call | solution.py:96
  101.1 3.4 %reshape.230 = bf16[64,2,2880]{2,1,0:T(2,128)(2,1)} reshape(bf16[192,1920]{1,0:T(8,128)(2,1)} %get-tuple-element.12) | data formatting | bytes 1474560 | tf_op jit(solution)/shard_map/reshape | solution.py:210
  104.5 13.8 %all-to-all-start.3 = ((bf16[64,2,2880]{2,1,0:T(2,128)(2,1)}), bf16[64,2,2880]{2,1,0:T(2,128)(2,1)S(1)}, u32[]{:S(2)}, u32[]{:S(2)}) async-start(bf16[64,2,2880]{2,1,0:T(2,128)(2,1)} %reshape.230), calls=%async_computation.3 | async-start | bytes 1507328 | tf_op jit(solution)/shard_map/all_to_all | solution.py:146
  118.3 2.0 %collective-permute-start.7 = (bf16[192,320]{1,0:T(8,128)(2,1)S(1)}, bf16[192,320]{1,0:T(8,128)(2,1)S(1)}, u32[]{:S(2)}, u32[]{:S(2)}) collective-permute-start(bf16[192,320]{1,0:T(8,128)(2,1)S(1)} %copy-done.6), channel_id=1, source_target_pairs={{0,8},{8,0},{1,9},{9,1},{2,10},{10,2},{3,11},{11,3},{4,12},{12,4},... | collective-permute-start | bytes 368648 | tf_op jit(solution)/shard_map/ppermute | solution.py:150
  120.3 1.2 collective-permute-done.7.got_ref
  121.5 1.8 shard_map.104
  123.3 4.2 %collective-permute-start.10 = (bf16[80,1280]{1,0:T(8,128)(2,1)S(1)}, bf16[80,1280]{1,0:T(8,128)(2,1)S(1)}, u32[]{:S(2)}, u32[]{:S(2)}) collective-permute-start(bf16[80,1280]{1,0:T(8,128)(2,1)S(1)} %get-tuple-element.18), channel_id=1, source_target_pairs={{0,256},{128,384},{256,0},{384,128},{1,257},{129,385},{257,1},{385... | collective-permute-start | bytes 614408 | tf_op jit(solution)/shard_map/ppermute | solution.py:150
  127.5 3.3 %collective-permute-start.11 = (bf16[80,1280]{1,0:T(8,128)(2,1)S(1)}, bf16[80,1280]{1,0:T(8,128)(2,1)S(1)}, u32[]{:S(2)}, u32[]{:S(2)}) collective-permute-start(bf16[80,1280]{1,0:T(8,128)(2,1)S(1)} %get-tuple-element.19), channel_id=1, source_target_pairs={{0,384},{128,0},{256,128},{384,256},{1,385},{129,1},{257,129},{385... | collective-permute-start | bytes 614408 | tf_op jit(solution)/shard_map/ppermute | solution.py:150
  130.8 2.6 %collective-permute-start.9 = (bf16[80,1280]{1,0:T(8,128)(2,1)S(1)}, bf16[80,1280]{1,0:T(8,128)(2,1)S(1)}, u32[]{:S(2)}, u32[]{:S(2)}) collective-permute-start(bf16[80,1280]{1,0:T(8,128)(2,1)S(1)} %get-tuple-element.17), channel_id=1, source_target_pairs={{0,128},{128,256},{256,384},{384,0},{1,129},{129,257},{257,385},{3... | collective-permute-start | bytes 614408 | tf_op jit(solution)/shard_map/ppermute | solution.py:150
  134.0 4.7 %collective-permute-done.10 = bf16[80,1280]{1,0:T(8,128)(2,1)S(1)} collective-permute-done((bf16[80,1280]{1,0:T(8,128)(2,1)S(1)}, bf16[80,1280]{1,0:T(8,128)(2,1)S(1)}, u32[]{:S(2)}, u32[]{:S(2)}) %collective-permute-start.10) | collective-permute-done | bytes 204832 | tf_op jit(solution)/shard_map/ppermute | solution.py:150
  138.7 4.2 %collective-permute-done.11 = bf16[80,1280]{1,0:T(8,128)(2,1)S(1)} collective-permute-done((bf16[80,1280]{1,0:T(8,128)(2,1)S(1)}, bf16[80,1280]{1,0:T(8,128)(2,1)S(1)}, u32[]{:S(2)}, u32[]{:S(2)}) %collective-permute-start.11) | collective-permute-done | bytes 204832 | tf_op jit(solution)/shard_map/ppermute | solution.py:150
  142.9 0.8 reshape.233
  143.7 6.3 %all-to-all-start.4 = ((bf16[8,2,6400]{2,1,0:T(2,128)(2,1)}), bf16[8,2,6400]{2,1,0:T(2,128)(2,1)S(1)}, u32[]{:S(2)}, u32[]{:S(2)}) async-start(bf16[8,2,6400]{2,1,0:T(2,128)(2,1)} %reshape.233), calls=%async_computation.4 | async-start | bytes 409600 | tf_op jit(solution)/shard_map/all_to_all | solution.py:146
  150.0 1.1 reshape.231
  151.1 1.1 fusion.1
  152.2 8.7 %all-to-all-done.4 = bf16[8,2,6400]{2,1,0:T(2,128)(2,1)S(1)} async-done(((bf16[8,2,6400]{2,1,0:T(2,128)(2,1)}), bf16[8,2,6400]{2,1,0:T(2,128)(2,1)S(1)}, u32[]{:S(2)}, u32[]{:S(2)}) %all-to-all-start.4) | async-done | bytes 204832 | tf_op jit(solution)/shard_map/all_to_all | solution.py:146
  161.1 0.8 broadcast_in_dim.8
  161.8 10.2 %all-to-all-start.5 = ((bf16[8,2,6400]{2,1,0:T(2,128)(2,1)}), bf16[8,2,6400]{2,1,0:T(2,128)(2,1)S(1)}, u32[]{:S(2)}, u32[]{:S(2)}) async-start(bf16[8,2,6400]{2,1,0:T(2,128)(2,1)} %broadcast_in_dim.8), calls=%async_computation.5 | async-start | bytes 409600 | tf_op jit(solution)/shard_map/all_to_all | solution.py:146
  172.0 2.6 %fusion.6 = bf16[1,3,64,1280]{3,1,2,0:T(4,128)(2,1)S(1)} fusion(f32[3,64]{0,1:T(8,128)S(1)} %broadcast_multiply_fusion, f32[3,64]{0,1:T(8,128)S(1)} %broadcast_multiply_fusion.2, f32[3,64]{0,1:T(8,128)S(1)} %broadcast_multiply_fusion.1, f32[1280]{0:T(1024)S(1)} %copy-done.5, f32[3,64]{0,1:T(8,128)S(1)} %add_rsqrt_fusion, bf16[1,3,64,1280]{3,2,1,0:T(8,128)(2,1)} %param.10, ...), kind=kLoop, calls=%fused_computation.16 | loop fusion | flops 2949120 | bytes 1974272 | tf_op jit(solution)/shard_map/broadcast_in_dim | solution.py:234
  174.8 0.8 copy.41
  175.6 0.6 copy-done.4
  176.3 1.3 fusion
  177.6 4.3 %all-to-all-done.5 = bf16[8,2,6400]{2,1,0:T(2,128)(2,1)S(1)} async-done(((bf16[8,2,6400]{2,1,0:T(2,128)(2,1)}), bf16[8,2,6400]{2,1,0:T(2,128)(2,1)S(1)}, u32[]{:S(2)}, u32[]{:S(2)}) %all-to-all-start.5) | async-done | bytes 204832 | tf_op jit(solution)/shard_map/all_to_all | solution.py:146
  182.0 0.7 reshape.234
  (41 shorter events, 2.6 us)
Async XLA Ops:
  2.2 33.4 %copy-start.3 = (bf16[1,3,64,1280]{3,2,1,0:T(8,128)(2,1)S(1)}, bf16[1,3,64,1280]{3,2,1,0:T(8,128)(2,1)}, u32[]{:S(2)}) copy-start(bf16[1,3,64,1280]{3,2,1,0:T(8,128)(2,1)} %param.10) | copy-start | bytes 1474564
  33.1 37.8 %copy-start.2 = (bf16[8,40,1280]{2,1,0:T(8,128)(2,1)}, bf16[8,40,1280]{2,1,0:T(8,128)(2,1)S(1)}, u32[]{:S(2)}) copy-start(bf16[8,40,1280]{2,1,0:T(8,128)(2,1)S(1)} %all_to_all.30.rest_0_) | copy-start | bytes 2457604
  33.1 24.7 %collective-permute-start.1 = (bf16[8,40,1280]{2,1,0:T(8,128)(2,1)S(1)}, bf16[8,40,1280]{2,1,0:T(8,128)(2,1)}, u32[]{:S(2)}, u32[]{:S(2)}) collective-permute-start(bf16[8,40,1280]{2,1,0:T(8,128)(2,1)S(1)} %all_to_all.30.rest_0_), channel_id=1, source_target_pairs={{0,384},{128,0},{256,128},{384,256},{1,385},{129,1},{257,129},{385... | collective-permute-start | bytes 2457608 | tf_op jit(solution)/shard_map/ppermute | solution.py:150
  36.0 8.4 %copy-start.1 = (bf16[1,3,64,1280]{3,2,1,0:T(8,128)(2,1)S(1)}, bf16[1,3,64,1280]{3,2,1,0:T(8,128)(2,1)}, u32[]{:S(2)}) copy-start(bf16[1,3,64,1280]{3,2,1,0:T(8,128)(2,1)} %param.8) | copy-start | bytes 1474564
  37.4 23.7 %copy-start.5 = (f32[1280]{0:T(1024)S(1)}, f32[1280]{0:T(1024)}, u32[]{:S(2)}) copy-start(f32[1280]{0:T(1024)} %param.11) | copy-start | bytes 15364
  37.4 25.7 %all-to-all-start.1 = ((bf16[64,2,1920]{2,1,0:T(2,128)(2,1)}), bf16[64,2,1920]{2,1,0:T(2,128)(2,1)S(1)}, u32[]{:S(2)}, u32[]{:S(2)}) async-start(bf16[64,2,1920]{2,1,0:T(2,128)(2,1)} %reshape.228), calls=%async_computation.1 | async-start | bytes 983040 | tf_op jit(solution)/shard_map/all_to_all | solution.py:146
  45.5 29.8 %collective-permute-start = (bf16[8,40,1280]{2,1,0:T(8,128)(2,1)S(1)}, bf16[8,40,1280]{2,1,0:T(8,128)(2,1)}, u32[]{:S(2)}, u32[]{:S(2)}) collective-permute-start(bf16[8,40,1280]{2,1,0:T(8,128)(2,1)S(1)} %all_to_all.30.rest_0_), channel_id=1, source_target_pairs={{0,128},{128,256},{256,384},{384,0},{1,129},{129,257},{257,385},{3... | collective-permute-start | bytes 2457608 | tf_op jit(solution)/shard_map/ppermute | solution.py:150
  57.8 19.6 %collective-permute-start.2 = (bf16[8,40,1280]{2,1,0:T(8,128)(2,1)}, bf16[8,40,1280]{2,1,0:T(8,128)(2,1)}, u32[]{:S(2)}, u32[]{:S(2)}) collective-permute-start(bf16[8,40,1280]{2,1,0:T(8,128)(2,1)} %collective-permute-done.1.rest_2_), channel_id=1, source_target_pairs={{0,384},{128,0},{256,128},{384,256},{1,385},{129,1},{257,129},{385... | collective-permute-start | bytes 2457608 | tf_op jit(solution)/shard_map/ppermute | solution.py:150
  63.0 24.2 %all-to-all-start = ((bf16[64,2,1920]{2,1,0:T(2,128)(2,1)}), bf16[64,2,1920]{2,1,0:T(2,128)(2,1)S(1)}, u32[]{:S(2)}, u32[]{:S(2)}) async-start(bf16[64,2,1920]{2,1,0:T(2,128)(2,1)} %reshape.226), calls=%async_computation | async-start | bytes 983040 | tf_op jit(solution)/shard_map/all_to_all | solution.py:146
  71.0 17.3 %collective-permute-start.3 = (bf16[8,40,1280]{2,1,0:T(8,128)(2,1)S(1)}, bf16[8,40,1280]{2,1,0:T(8,128)(2,1)}, u32[]{:S(2)}, u32[]{:S(2)}) collective-permute-start(bf16[8,40,1280]{2,1,0:T(8,128)(2,1)S(1)} %all_to_all.30.rest_0_), channel_id=1, source_target_pairs={{0,8},{8,0},{1,9},{9,1},{2,10},{10,2},{3,11},{11,3},{4,12},{12,4},... | collective-permute-start | bytes 2457608 | tf_op jit(solution)/shard_map/ppermute | solution.py:150
  73.0 15.3 %collective-permute-start.5 = (bf16[8,40,1280]{2,1,0:T(8,128)(2,1)}, bf16[8,40,1280]{2,1,0:T(8,128)(2,1)}, u32[]{:S(2)}, u32[]{:S(2)}) collective-permute-start(bf16[8,40,1280]{2,1,0:T(8,128)(2,1)} %collective-permute-done.1.rest_2_), channel_id=1, source_target_pairs={{0,8},{8,0},{1,9},{9,1},{2,10},{10,2},{3,11},{11,3},{4,12},{12,4},... | collective-permute-start | bytes 2457608 | tf_op jit(solution)/shard_map/ppermute | solution.py:150
  75.3 13.0 %collective-permute-start.4 = (bf16[8,40,1280]{2,1,0:T(8,128)(2,1)}, bf16[8,40,1280]{2,1,0:T(8,128)(2,1)}, u32[]{:S(2)}, u32[]{:S(2)}) collective-permute-start(bf16[8,40,1280]{2,1,0:T(8,128)(2,1)} %collective-permute-done.rest_1_), channel_id=1, source_target_pairs={{0,8},{8,0},{1,9},{9,1},{2,10},{10,2},{3,11},{11,3},{4,12},{12,4},... | collective-permute-start | bytes 2457608 | tf_op jit(solution)/shard_map/ppermute | solution.py:150
  77.4 10.9 %collective-permute-start.6 = (bf16[8,40,1280]{2,1,0:T(8,128)(2,1)}, bf16[8,40,1280]{2,1,0:T(8,128)(2,1)}, u32[]{:S(2)}, u32[]{:S(2)}) collective-permute-start(bf16[8,40,1280]{2,1,0:T(8,128)(2,1)} %collective-permute-done.2.rest_3_), channel_id=1, source_target_pairs={{0,8},{8,0},{1,9},{9,1},{2,10},{10,2},{3,11},{11,3},{4,12},{12,4},... | collective-permute-start | bytes 2457608 | tf_op jit(solution)/shard_map/ppermute | solution.py:150
  84.4 35.9 %collective-permute-start.8 = (bf16[192,1280]{1,0:T(8,128)(2,1)}, bf16[192,1280]{1,0:T(8,128)(2,1)S(1)}, u32[]{:S(2)}, u32[]{:S(2)}) collective-permute-start(bf16[192,1280]{1,0:T(8,128)(2,1)} %reshape.229.grad_ref), channel_id=1, source_target_pairs={{0,8},{8,0},{1,9},{9,1},{2,10},{10,2},{3,11},{11,3},{4,12},{12,4},... | collective-permute-start | bytes 1474568 | tf_op jit(solution)/shard_map/ppermute | solution.py:150
  101.1 17.2 %copy-start.6 = (bf16[192,320]{1,0:T(8,128)(2,1)S(1)}, bf16[192,320]{1,0:T(8,128)(2,1)}, u32[]{:S(2)}) copy-start(bf16[192,320]{1,0:T(8,128)(2,1)} %get-tuple-element.15) | copy-start | bytes 368644
  101.1 20.4 %copy-start = (bf16[192,320]{1,0:T(8,128)(2,1)S(1)}, bf16[192,320]{1,0:T(8,128)(2,1)}, u32[]{:S(2)}) copy-start(bf16[192,320]{1,0:T(8,128)(2,1)} %get-tuple-element.14.own_ref) | copy-start | bytes 368644
  104.5 39.2 %all-to-all-start.3 = ((bf16[64,2,2880]{2,1,0:T(2,128)(2,1)}), bf16[64,2,2880]{2,1,0:T(2,128)(2,1)S(1)}, u32[]{:S(2)}, u32[]{:S(2)}) async-start(bf16[64,2,2880]{2,1,0:T(2,128)(2,1)} %reshape.230), calls=%async_computation.3 | async-start | bytes 1507328 | tf_op jit(solution)/shard_map/all_to_all | solution.py:146
  118.3 3.3 %collective-permute-start.7 = (bf16[192,320]{1,0:T(8,128)(2,1)S(1)}, bf16[192,320]{1,0:T(8,128)(2,1)S(1)}, u32[]{:S(2)}, u32[]{:S(2)}) collective-permute-start(bf16[192,320]{1,0:T(8,128)(2,1)S(1)} %copy-done.6), channel_id=1, source_target_pairs={{0,8},{8,0},{1,9},{9,1},{2,10},{10,2},{3,11},{11,3},{4,12},{12,4},... | collective-permute-start | bytes 368648 | tf_op jit(solution)/shard_map/ppermute | solution.py:150
  123.3 15.3 %collective-permute-start.10 = (bf16[80,1280]{1,0:T(8,128)(2,1)S(1)}, bf16[80,1280]{1,0:T(8,128)(2,1)S(1)}, u32[]{:S(2)}, u32[]{:S(2)}) collective-permute-start(bf16[80,1280]{1,0:T(8,128)(2,1)S(1)} %get-tuple-element.18), channel_id=1, source_target_pairs={{0,256},{128,384},{256,0},{384,128},{1,257},{129,385},{257,1},{385... | collective-permute-start | bytes 614408 | tf_op jit(solution)/shard_map/ppermute | solution.py:150
  127.5 15.3 %collective-permute-start.11 = (bf16[80,1280]{1,0:T(8,128)(2,1)S(1)}, bf16[80,1280]{1,0:T(8,128)(2,1)S(1)}, u32[]{:S(2)}, u32[]{:S(2)}) collective-permute-start(bf16[80,1280]{1,0:T(8,128)(2,1)S(1)} %get-tuple-element.19), channel_id=1, source_target_pairs={{0,384},{128,0},{256,128},{384,256},{1,385},{129,1},{257,129},{385... | collective-permute-start | bytes 614408 | tf_op jit(solution)/shard_map/ppermute | solution.py:150
  130.8 12.1 %collective-permute-start.9 = (bf16[80,1280]{1,0:T(8,128)(2,1)S(1)}, bf16[80,1280]{1,0:T(8,128)(2,1)S(1)}, u32[]{:S(2)}, u32[]{:S(2)}) collective-permute-start(bf16[80,1280]{1,0:T(8,128)(2,1)S(1)} %get-tuple-element.17), channel_id=1, source_target_pairs={{0,128},{128,256},{256,384},{384,0},{1,129},{129,257},{257,385},{3... | collective-permute-start | bytes 614408 | tf_op jit(solution)/shard_map/ppermute | solution.py:150
  143.7 17.2 %all-to-all-start.4 = ((bf16[8,2,6400]{2,1,0:T(2,128)(2,1)}), bf16[8,2,6400]{2,1,0:T(2,128)(2,1)S(1)}, u32[]{:S(2)}, u32[]{:S(2)}) async-start(bf16[8,2,6400]{2,1,0:T(2,128)(2,1)} %reshape.233), calls=%async_computation.4 | async-start | bytes 409600 | tf_op jit(solution)/shard_map/all_to_all | solution.py:146
  161.8 20.0 %all-to-all-start.5 = ((bf16[8,2,6400]{2,1,0:T(2,128)(2,1)}), bf16[8,2,6400]{2,1,0:T(2,128)(2,1)S(1)}, u32[]{:S(2)}, u32[]{:S(2)}) async-start(bf16[8,2,6400]{2,1,0:T(2,128)(2,1)} %broadcast_in_dim.8), calls=%async_computation.5 | async-start | bytes 409600 | tf_op jit(solution)/shard_map/all_to_all | solution.py:146
  174.7 1.6 copy-start.4
